TPU v7x, 32 devices: a whole 2x2x4 slice. The times are simulated.
32 devices in a mesh: freq: 4 (over y, core), row: 4 (over z), col: 2 (over x).
Axes of the slice: x: 2, y: 2, z: 4, core: 2. Of those that a mesh axis runs over, the one named last changes fastest.
Arguments:
- voltages: bfloat16 [128, 259, 2048], P(('row', 'col', 'freq')), may hold values from -128 to 127, as said below
- tap_table: int32 [4, 2048], replicated, may hold values from -4096 to 4095
Outputs:
- visibility: float32 [1024, 2, 4, 32, 128], P('freq', None, None, 'col', 'row')
Inputs may be any that keep to these rules, and one draw needn't show every extreme that they name: `voltages`: whole numbers.
All inputs are finite; a program needn't handle non-finite values.
Results may differ from a plain program's by a relative error of at most 0.0033.
Values may be sent and summed in bfloat16 or wider, within the bound.
No kernel may reach another device: no remote copies, remote signals or barrier semaphores. Data moves between devices by JAX's collectives and lax.ppermute only.
A program may use at most 192 MiB of HBM per device.

v0:
```python
import functools
import math

import jax
import jax.numpy as jnp
import numpy as np
from jax import lax
from jax.experimental import pallas as pl
from jax.experimental.pallas import tpu as pltpu
from jax.sharding import PartitionSpec as P


OWNERS = ("col", "row")
EVERYONE = ("col", "row", "freq")
ROWS_ALIKE = (((1,), (1,)), ((), ()))
WHOLE = pl.BlockSpec(memory_space=pltpu.VMEM)
ANYWHERE = pl.BlockSpec(memory_space=pl.ANY)
SCALARS = pl.BlockSpec(memory_space=pltpu.SMEM)

FOURS = (0, 4, ((1, 1, 1, 1),))
TWOS = (2, 4, ((1, -1, 1, -1),))
ODDS = (1, 2, ((1, 0, -1, 0), (0, 1, 0, -1)))
CHUNKS = ((FOURS,), (TWOS, ODDS))
PAD = 8


def split(value):
    high = value.astype(jnp.bfloat16)
    low = (value - high.astype(jnp.float32)).astype(jnp.bfloat16)
    return high, low


def angle_tables(length, channels, kind):
    residue, modulus, folds = kind
    stride = 2 ** ((channels.bit_length() - 1) // 2)
    sample = np.arange(length // 4 * len(folds))
    factor = 1.0 / (64.0 * math.sqrt(length))
    coarse = 2.0 * math.pi / length * ((np.arange(0, channels, stride)[:, None] * sample) % length)
    fine = 2.0 * math.pi / length * ((np.arange(residue, stride, modulus)[:, None] * sample) % length)
    coarse = np.stack([np.cos(coarse), np.sin(coarse)]) * factor
    fine = np.stack([np.cos(fine), np.sin(fine)])
    return jnp.asarray(coarse, jnp.float32), jnp.asarray(fine, jnp.float32)


def signed_sum(values, signs):
    total = None
    for value, sign in zip(values, signs):
        if sign:
            total = value * sign if total is None else (total + value if sign > 0 else total - value)
    return total


def dft_kernel(kinds, rows_apart, me, source, taps, *refs):
    tables, outs, scratch = refs[: 2 * len(kinds)], refs[2 * len(kinds) :][: rows_apart or 1], refs[2 * len(kinds) :]
    out, volts, sem, fold = scratch[len(outs) : len(outs) + 4]
    scratch = scratch[len(outs) + 4 :]
    frames, inputs, length = volts.shape
    quarter = length // 4
    tap_count = taps.shape[0]
    spec_count = frames - tap_count + 1
    step, lanes, stages = 16, 128, sem.shape[0]
    rows, tiles = step * inputs, quarter // lanes
    bounds = [spec_count * x // stages + (tap_count - 1 if x else 0) for x in range(stages + 1)]
    copies = []
    for x in range(stages):
        part = pl.ds(bounds[x], bounds[x + 1] - bounds[x])
        copies.append(pltpu.make_async_copy(source.at[part], volts.at[part], sem.at[x, 0]))
        copies[-1].start()

    def filter_rows(index, carry):
        for tile in range(tiles):
            values = []
            for x in range(4):
                at = pl.ds(x * quarter + tile * lanes, lanes)
                weight = taps[:, at].astype(jnp.float32) / 4096.0
                block = volts[pl.ds(index * step, step + tap_count - 1), :, at].astype(jnp.float32).reshape(-1, lanes)
                value = weight[0:1] * block[:rows]
                for k in range(1, tap_count):
                    value = value + weight[k : k + 1] * block[k * inputs : k * inputs + rows]
                values.append(value)
            piece = 0
            for _, _, folds in kinds:
                for signs in folds:
                    at = pl.ds(pl.multiple_of(index * rows, rows), rows)
                    fold[piece * tiles + tile, at, :] = signed_sum(values, signs)
                    piece += 1
        return carry

    for x in range(stages):
        copies[x].wait()
        lax.fori_loop(spec_count * x // stages // step, spec_count * (x + 1) // stages // step, filter_rows, 0)
    piece = 0
    for x, (_, _, folds) in enumerate(kinds):
        high, low = scratch[4 * x : 4 * x + 2]
        for y in range(len(folds)):
            for tile in range(tiles):
                for i in range(inputs):
                    at = pl.ds(i * spec_count, spec_count), pl.ds(y * quarter + tile * lanes, lanes)
                    high[at], low[at] = split(fold[piece, pl.ds(i, spec_count, stride=inputs), :])
                piece += 1

    dot = functools.partial(lax.dot_general, dimension_numbers=ROWS_ALIKE, preferred_element_type=jnp.float32)
    owners, groups, _, _, _ = out.shape
    slot = 0
    for x in range(len(kinds)):
        coarse, fine = tables[2 * x : 2 * x + 2]
        high, low, table_high, table_low = scratch[4 * x : 4 * x + 4]
        channels = table_high.shape[0] // 2
        fine_count = fine.shape[1]
        for a in range(channels // fine_count):
            cos_a, sin_a = coarse[0, a : a + 1], coarse[1, a : a + 1]
            real = cos_a * fine[0] - sin_a * fine[1]
            imag = -(sin_a * fine[0]) - cos_a * fine[1]
            for part, value in enumerate((real, imag)):
                at = pl.ds(part * channels + a * fine_count, fine_count)
                table_high[at], table_low[at] = split(value)
        result = dot(table_high[...], high[...]) + (dot(table_high[...], low[...]) + dot(table_low[...], high[...]))
        result = result.astype(jnp.bfloat16)
        each = channels // groups // owners
        for part in range(2):
            for group in range(groups):
                for owner in range(owners):
                    start = ((part * groups + group) * owners + owner) * each
                    out[owner, group, part, slot : slot + each] = result[start : start + each]
        slot += each
    if rows_apart:
        row_of = [lax.rem(me[1] + k, rows_apart) for k in range(rows_apart)]
        copies = [
            pltpu.make_async_copy(out.at[pl.ds(col * rows_apart + row, 1)], outs[k].at[pl.ds(col, 1)], sem.at[k, col])
            for k, row in enumerate(row_of)
            for col in range(owners // rows_apart)
        ]
    else:
        copies = [pltpu.make_async_copy(out, outs[0], sem.at[0, 0])]
    for copy in copies:
        copy.start()
    for copy in copies:
        copy.wait()


def dft(volts, taps, me, kinds, groups, owners, rows_apart):
    frames, inputs, length = volts.shape
    width = inputs * (frames - taps.shape[0] + 1)
    channels = length // 2
    operands, scratch, count, pieces, flops = [me, volts, taps], [], 0, 0, 0
    for kind in kinds:
        _, modulus, folds = kind
        operands += angle_tables(length, channels, kind)
        folded, rows = length // 4 * len(folds), 2 * channels // modulus
        scratch += [pltpu.VMEM((width, folded), jnp.bfloat16)] * 2 + [pltpu.VMEM((rows, folded), jnp.bfloat16)] * 2
        count += channels // modulus // groups // owners
        pieces += len(folds)
        flops += 6 * rows * folded * width
    shape = (owners, groups, 2, count, width)
    out_shape = jax.ShapeDtypeStruct((owners // (rows_apart or 1),) + shape[1:] if rows_apart else shape, jnp.bfloat16)
    return pl.pallas_call(
        functools.partial(dft_kernel, kinds, rows_apart),
        in_specs=[SCALARS, ANYWHERE] + [WHOLE] * (len(operands) - 2),
        out_specs=[ANYWHERE] * (rows_apart or 1),
        out_shape=[out_shape] * (rows_apart or 1),
        scratch_shapes=[
            pltpu.VMEM(shape, jnp.bfloat16),
            pltpu.VMEM(volts.shape, volts.dtype),
            pltpu.SemaphoreType.DMA((4, owners)),
            pltpu.VMEM((pieces * (length // 4 // 128), width, 128), jnp.float32),
            *scratch,
        ],
        cost_estimate=pl.CostEstimate(
            flops=flops, bytes_accessed=2 * frames * inputs * length + 2 * math.prod(shape), transcendentals=0
        ),
    )(*operands)


def turn_kernel(me, *refs):
    sem = refs[-1]
    plane, rows = sem.shape
    blocks, outs = refs[:rows], refs[rows:-1]
    copies = []
    for q in range(plane):
        to = lax.rem(me[2] + q, plane)
        for k in range(rows):
            origin = lax.rem(me[1] + (rows - k), rows)
            copies.append(pltpu.make_async_copy(blocks[k].at[to], outs[q].at[origin], sem.at[q, k]))
    for copy in copies:
        copy.start()
    for copy in copies:
        copy.wait()


def turn(blocks, me):
    plane, rows = blocks[0].shape[0], len(blocks)
    shape = jax.ShapeDtypeStruct((rows,) + blocks[0].shape[1:], jnp.bfloat16)
    return pl.pallas_call(
        turn_kernel,
        in_specs=[SCALARS] + [WHOLE] * rows,
        out_specs=[ANYWHERE] * plane,
        out_shape=[shape] * plane,
        scratch_shapes=[pltpu.SemaphoreType.DMA((plane, rows))],
    )(me, *blocks)


def correlate_kernel(sizes, count, me, *refs):
    cols, rows, groups, inputs = sizes
    sources = cols * rows * groups
    out, scratch, sem = refs[-2], refs[-3], refs[-1]
    apart = refs[0].shape[0] == rows
    got, outs = (refs[: cols * groups], refs[cols * groups : -3]) if apart else (refs[0], refs[1:-3])
    width = scratch.shape[0] // 2 * 128
    spec_count = width // inputs
    tiles = width // 128
    for part in range(2):
        for tile in range(tiles):
            lanes = slice(tile * 128, (tile + 1) * 128)
            if not apart:
                scratch[part * tiles + tile] = got[:, part, :, lanes].astype(jnp.float32).reshape(sources * count, 128)
                continue
            for q, block in enumerate(got):
                origin = lax.rem(me[2] + (cols * groups - q), cols * groups)
                col, group = origin // groups, lax.rem(origin, groups)
                for row in range(rows):
                    at = pl.multiple_of(((col * rows + row) * groups + group) * count, 8)
                    scratch[part * tiles + tile, pl.ds(at, count), :] = block[row, part, :, lanes].astype(jnp.float32)

    def one_channel(k, carry):
        loaded = [scratch[x, pl.ds(k, sources, stride=count), :].astype(jnp.bfloat16) for x in range(2 * tiles)]
        each = tiles // inputs
        parts = [jnp.concatenate(loaded[x * each : (x + 1) * each], axis=1) for x in range(2 * inputs)]
        real, imag = parts[:inputs], parts[inputs:]
        left = jnp.concatenate([jnp.concatenate(x, axis=0) for x in (real, imag)], axis=1)
        near, far = [], []
        for col in range(cols):
            at = slice(col * rows * groups, (col + 1) * rows * groups)
            near += [x[at] for x in real] + [-x[at] for x in imag]
            far += [x[at] for x in imag] + [x[at] for x in real]
        right = jnp.concatenate([jnp.concatenate(near, axis=0), jnp.concatenate(far, axis=0)], axis=1)
        value = lax.dot_general(left, right, ROWS_ALIKE, preferred_element_type=jnp.float32) * (1.0 / spec_count)
        lanes = value.shape[1] // cols
        for row in range(rows):
            picked = jnp.concatenate(
                [value[(x * rows + row) * groups : (x * rows + row + 1) * groups] for x in range(inputs * cols)], axis=0
            ).astype(jnp.bfloat16)
            for col in range(cols):
                out[col * rows + row, k] = picked[:, col * lanes : (col + 1) * lanes]
        return carry

    lax.fori_loop(0, count, one_channel, 0, unroll=2)
    owners = cols * rows
    if len(outs) == 1:
        copies = [pltpu.make_async_copy(out, outs[0], sem.at[0])]
    else:
        copies = [pltpu.make_async_copy(out.at[lax.rem(me[0] + k, owners)], outs[k], sem.at[k]) for k in range(owners)]
    for copy in copies:
        copy.start()
    for copy in copies:
        copy.wait()


def correlate(got, me, sizes, apart):
    cols, rows, groups, inputs = sizes
    sources = cols * rows * groups
    count, width = got[0].shape[-2:]
    block = groups * inputs
    shape = (cols * rows, count, cols * block, 2 * rows * block)
    return pl.pallas_call(
        functools.partial(correlate_kernel, sizes, count),
        in_specs=[SCALARS] + [WHOLE] * len(got),
        out_specs=[pl.BlockSpec(memory_space=pl.ANY)] * (shape[0] if apart else 1),
        out_shape=[jax.ShapeDtypeStruct(shape[1:] if apart else shape, jnp.bfloat16)] * (shape[0] if apart else 1),
        scratch_shapes=[
            pltpu.VMEM((2 * width // 128, sources * count, 128), jnp.float32),
            pltpu.VMEM(shape, jnp.bfloat16),
            pltpu.SemaphoreType.DMA((shape[0],)),
        ],
        cost_estimate=pl.CostEstimate(
            flops=8 * count * sources * inputs * sources * width,
            bytes_accessed=4 * sources * count * width + 2 * math.prod(shape),
            transcendentals=0,
        ),
    )(me, *got)


def places(count_of):
    result = []
    for kinds in CHUNKS:
        result.append([residue + modulus * x for residue, modulus, _ in kinds for x in range(count_of(modulus))])
    return result


def finish_kernel(sizes, me, first, *refs):
    pieces, (same, out, scratch, held, sem) = refs[:-5], refs[-5:]
    cols, rows, groups, inputs = sizes
    owners, _, width, lanes = first.shape
    total = first.shape[1] + pieces[0].shape[0]
    tiles = lanes // 128
    pitch = scratch.shape[1] // (owners * total)
    whole = [(k, first.at[k], 0) for k in range(owners)]
    whole += [(lax.rem(me[0] + (owners - k), owners), piece, 1) for k, piece in enumerate(pieces)]
    slots_of = places(lambda modulus: total // modulus)
    for owner, got, chunk in whole:
        for slot, place in enumerate(slots_of[chunk]):
            for tile in range(tiles):
                value = got[slot, :, tile * 128 : (tile + 1) * 128].astype(jnp.float32)
                at = pl.multiple_of((owner * total + place) * pitch, 8)
                scratch[tile, pl.ds(at, width), :] = value

    flat = held.reshape(held.shape[0], held.shape[1] * held.shape[2], 128)

    copies = []
    for half in range(held.shape[0]):

        def one_row(x, carry):
            i, rest = x // (cols * groups), x % (cols * groups)
            at = rest * inputs + i
            for tile in range(tiles):
                rows_of = pl.ds(half * 128 * pitch + x, 128, stride=pitch)
                block = scratch[tile, rows_of, :].astype(jnp.bfloat16)
                value = lax.dot_general(same[...], block, ROWS_ALIKE, preferred_element_type=jnp.float32)
                for y in range(128 // (rows * groups)):
                    part, j = divmod(tile * (128 // (rows * groups)) + y, inputs)
                    start = part * rows * groups * held.shape[2] + j * width + at
                    piece = value[y * rows * groups : (y + 1) * rows * groups]
                    flat[half, pl.ds(start, rows * groups, stride=held.shape[2]), :] = piece
            return carry

        lax.fori_loop(0, width, one_row, 0, unroll=32)
        copies.append(
            pltpu.make_async_copy(
                held.at[half, :, pl.ds(0, out.shape[1])], out.at[:, :, pl.ds(half * 128, 128)], sem.at[half]
            )
        )
        copies[-1].start()
    for copy in copies:
        copy.wait()


def finish(first, pieces, me, sizes):
    cols, rows, groups, inputs = sizes
    owners, _, width, lanes = first.shape
    total = first.shape[1] + pieces[0].shape[0]
    channels = owners * total
    if channels % 128 or 128 % (rows * groups):
        order = np.argsort(sum(places(lambda modulus: total // modulus), []))
        second = jnp.stack(pieces)[(me[0] - jnp.arange(owners)) % owners]
        value = jnp.concatenate([first, second], axis=1)[:, order]
        value = value.reshape(channels, inputs, cols, groups, 2, inputs, rows, groups)
        return value.transpose(4, 6, 7, 5, 2, 3, 1, 0).reshape(lanes * width, channels).astype(jnp.float32)
    return pl.pallas_call(
        functools.partial(finish_kernel, sizes),
        in_specs=[pl.BlockSpec(memory_space=pltpu.SMEM)] + [WHOLE] * (owners + 2),
        out_specs=pl.BlockSpec(memory_space=pl.ANY),
        out_shape=jax.ShapeDtypeStruct((2 * rows * groups, inputs * width, channels), jnp.float32),
        scratch_shapes=[
            pltpu.VMEM((lanes // 128, channels * (width + PAD), 128), jnp.float32),
            pltpu.VMEM((channels // 128, 2 * rows * groups, inputs * width + PAD, 128), jnp.float32),
            pltpu.SemaphoreType.DMA((channels // 128,)),
        ],
    )(me, first, *pieces, jnp.eye(128, dtype=jnp.bfloat16))


def shards(voltages, tap_table):
    groups, rows, cols = (lax.axis_size(name) for name in ("freq", "row", "col"))
    inputs = voltages.shape[0]
    sizes = (cols, rows, groups, inputs)
    volts = voltages.transpose(1, 0, 2)
    owners = rows * cols
    plane = cols * groups
    row, col, group = (lax.axis_index(name) for name in ("row", "col", "freq"))
    me = jnp.stack([col * rows + row, row, col * groups + group]).astype(jnp.int32)

    blocks = list(dft(volts, tap_table, me, CHUNKS[0], groups, owners, rows))
    for k in range(1, rows):
        blocks[k] = lax.ppermute(blocks[k], "row", [(x, (x + k) % rows) for x in range(rows)])
    sent = dft(volts, tap_table, me, CHUNKS[1], groups, owners, 0)[0]
    sent = sent.reshape((-1,) + sent.shape[2:])
    second = lax.all_to_all(sent, EVERYONE, split_axis=0, concat_axis=0, tiled=True)
    blocks = list(turn([x.reshape((plane,) + x.shape[2:]) for x in blocks], me))
    meshed = lambda place: place % groups * cols + place // groups
    for q in range(1, plane):
        pairs = [(meshed(x), meshed((x + q) % plane)) for x in range(plane)]
        blocks[q] = lax.ppermute(blocks[q], ("freq", "col"), pairs)
    if blocks[0].shape[2] % 8:
        stacked = jnp.stack(blocks)[(me[2] - jnp.arange(plane)) % plane]
        stacked = stacked.reshape((cols, groups) + stacked.shape[1:]).swapaxes(1, 2)
        blocks = [stacked.reshape((-1,) + stacked.shape[3:])]

    first = correlate(blocks, me, sizes, False)[0]
    first = lax.all_to_all(first, OWNERS, split_axis=0, concat_axis=0, tiled=True)
    pieces = list(correlate([second], me, sizes, True))
    meshed = lambda owner: owner % rows * cols + owner // rows
    for k in range(1, owners):
        pairs = [(meshed(x), meshed((x + k) % owners)) for x in range(owners)]
        pieces[k] = lax.ppermute(pieces[k], OWNERS[::-1], pairs)
    result = finish(first, pieces, me, sizes)
    block = groups * inputs
    return result.reshape(2, rows, block, cols * block, -1).transpose(4, 0, 1, 2, 3)


def solution(mesh):
    in_specs = (P(("row", "col", "freq"), None, None), P())
    out_specs = P("freq", None, None, "col", "row")
    return jax.shard_map(shards, mesh=mesh, in_specs=in_specs, out_specs=out_specs, check_vma=False)
```

profile of v0, /device:TPU:0, one launch (start us, length us, event | category | flops | bytes accessed | tf_op | source)
XLA Modules:
  0.0 198.6 jit_solution(14202656454851824366)
XLA Ops:
  0.7 17.3 %shard_map.85 = bf16[8,4,2,24,1024]{4,3,2,1,0:T(8,128)(2,1)} custom-call(s32[3]{0:T(128)} %pad_add_fusion.me, bf16[259,4,2048]{2,1,0:T(4,128)(2,1)} %bitcast.15, s32[4,2048]{1,0:T(4,128)} %taps.3, f32[2,32,512]{2,1,0:T(8,128)} %constant.23.clone.refs_0_, f32[2,8,512]{2,1,0:T(8,128)} %constant.25.clone.refs_1_, f32[2,32,1024]{2,1,0:T(8,128)} %constant.26.clone.refs_2_, ...), custom_call_target="tpu_custom_call" | custom-call | flops 8053063680 | bytes 7389184 | tf_op jit(solution)/shard_map/pallas_call | solution.py:156
  17.9 7.3 %all-to-all-start.1 = ((bf16[32,2,24,1024]{3,2,1,0:T(8,128)(2,1)}), bf16[32,2,24,1024]{3,2,1,0:T(8,128)(2,1)S(1)}, u32[]{:S(2)}, u32[]{:S(2)}) async-start(bf16[32,2,24,1024]{3,2,1,0:T(8,128)(2,1)} %bitcast.12), calls=%async_computation.1 | async-start | bytes 6291456 | tf_op jit(solution)/shard_map/all_to_all | solution.py:375
  25.2 9.0 %shard_map.82 = (bf16[2,4,2,8,1024]{4,3,2,1,0:T(8,128)(2,1)}, bf16[2,4,2,8,1024]{4,3,2,1,0:T(8,128)(2,1)}, bf16[2,4,2,8,1024]{4,3,2,1,0:T(8,128)(2,1)}, bf16[2,4,2,8,1024]{4,3,2,1,0:T(8,128)(2,1)}) custom-call(s32[3]{0:T(128)} %pad_add_fusion.me, bf16[259,4,2048]{2,1,0:T(4,128)(2,1)} %bitcast.16, s32[4,2048]{1,0:T(4,128)} %taps.3, ...), custom_call_target="tpu_custom_call" | custom-call | flops 1610612736 | bytes 5292032 | tf_op jit(solution)/shard_map/pallas_call | solution.py:156
  34.3 1.8 collective-permute-start
  36.1 2.4 %collective-permute-start.1 = (bf16[2,4,2,8,1024]{4,3,2,1,0:T(8,128)(2,1)}, bf16[2,4,2,8,1024]{4,3,2,1,0:T(8,128)(2,1)}, u32[]{:S(2)}, u32[]{:S(2)}) collective-permute-start(bf16[2,4,2,8,1024]{4,3,2,1,0:T(8,128)(2,1)} %get-tuple-element.27), channel_id=1, source_target_pairs={{0,4},{2,6},{4,0},{6,2},{1,5},{3,7},{5,1},{7,3},{8,12},{10,14},{12... | collective-permute-start | bytes 786440 | tf_op jit(solution)/shard_map/ppermute | solution.py:372
  40.0 47.8 %collective-permute-done = bf16[2,4,2,8,1024]{4,3,2,1,0:T(8,128)(2,1)S(1)} collective-permute-done((bf16[2,4,2,8,1024]{4,3,2,1,0:T(8,128)(2,1)}, bf16[2,4,2,8,1024]{4,3,2,1,0:T(8,128)(2,1)S(1)}, u32[]{:S(2)}, u32[]{:S(2)}) %collective-permute-start) | collective-permute-done | bytes 262176 | tf_op jit(solution)/shard_map/ppermute | solution.py:372
  87.8 26.9 %collective-permute-done.1 = bf16[2,4,2,8,1024]{4,3,2,1,0:T(8,128)(2,1)} collective-permute-done((bf16[2,4,2,8,1024]{4,3,2,1,0:T(8,128)(2,1)}, bf16[2,4,2,8,1024]{4,3,2,1,0:T(8,128)(2,1)}, u32[]{:S(2)}, u32[]{:S(2)}) %collective-permute-start.1) | collective-permute-done | bytes 262176 | tf_op jit(solution)/shard_map/ppermute | solution.py:372
  114.7 2.5 %shard_map.83 = (bf16[4,2,8,1024]{3,2,1,0:T(8,128)(2,1)}, bf16[4,2,8,1024]{3,2,1,0:T(8,128)(2,1)}, bf16[4,2,8,1024]{3,2,1,0:T(8,128)(2,1)}, bf16[4,2,8,1024]{3,2...) custom-call(s32[3]{0:T(128)} %pad_add_fusion.me, ...), custom_call_target="tpu_custom_call" | custom-call | tf_op jit(solution)/shard_map/pallas_call | solution.py:193
  118.1 2.3 %collective-permute-start.5 = (bf16[4,2,8,1024]{3,2,1,0:T(8,128)(2,1)}, bf16[4,2,8,1024]{3,2,1,0:T(8,128)(2,1)S(1)}, u32[]{:S(2)}, u32[]{:S(2)}) collective-permute-start(bf16[4,2,8,1024]{3,2,1,0:T(8,128)(2,1)} %get-tuple-element.32), channel_id=1, source_target_pairs={{0,24},{8,1},{16,9},{24,17},{1,25},{9,0},{17,8},{25,16},{2,26},{10... | collective-permute-start | bytes 393224 | tf_op jit(solution)/shard_map/ppermute | solution.py:380
  121.1 2.4 %collective-permute-done.3.refs_1_ = bf16[4,2,8,1024]{3,2,1,0:T(8,128)(2,1)S(1)} collective-permute-done((bf16[4,2,8,1024]{3,2,1,0:T(8,128)(2,1)}, bf16[4,2,8,1024]{3,2,1,0:T(8,128)(2,1)S(1)}, u32[]{:S(2)}, u32[]{:S(2)}) %collective-permute-start.3) | collective-permute-done | bytes 131104 | tf_op jit(solution)/shard_map/ppermute | solution.py:380
  124.8 1.8 collective-permute-start.9
  126.6 2.7 %collective-permute-done.7.refs_5_ = bf16[4,2,8,1024]{3,2,1,0:T(8,128)(2,1)} collective-permute-done((bf16[4,2,8,1024]{3,2,1,0:T(8,128)(2,1)}, bf16[4,2,8,1024]{3,2,1,0:T(8,128)(2,1)}, u32[]{:S(2)}, u32[]{:S(2)}) %collective-permute-start.7) | collective-permute-done | bytes 131104 | tf_op jit(solution)/shard_map/ppermute | solution.py:380
  131.7 4.1 %shard_map.84 = bf16[8,8,32,128]{3,2,1,0:T(8,128)(2,1)} custom-call(s32[3]{0:T(128)} %pad_add_fusion.me, bf16[4,2,8,1024]{3,2,1,0:T(8,128)(2,1)} %get-tuple-element.29.refs_0_, bf16[4,2,8,1024]{3,2,1,0:T(8,128)(2,1)} %copy-done.9, bf16[4,2,8,1024]{3,2,1,0:T(8,128)(2,1)} %copy-done.10, bf16[4,2,8,1024]{3,2,1,0:T(8,128)(2,1)} %copy-done.11, ...), custom_call_target="tpu_custom_call" | custom-call | flops 268435456 | bytes 1572864 | tf_op jit(solution)/shard_map/pallas_call | solution.py:264
  135.8 7.8 %all-to-all-start = ((bf16[8,8,32,128]{3,2,1,0:T(8,128)(2,1)}), bf16[8,8,32,128]{3,2,1,0:T(8,128)(2,1)}, u32[]{:S(2)}, u32[]{:S(2)}) async-start(bf16[8,8,32,128]{3,2,1,0:T(8,128)(2,1)} %shard_map.84), calls=%async_computation | async-start | bytes 1048576 | tf_op jit(solution)/shard_map/all_to_all | solution.py:387
  143.6 7.6 %shard_map.86 = (bf16[24,32,128]{2,1,0:T(8,128)(2,1)}, bf16[24,32,128]{2,1,0:T(8,128)(2,1)}, bf16[24,32,128]{2,1,0:T(8,128)(2,1)}, bf16[24,32,128]{2,1,0:T(8,128...) custom-call(s32[3]{0:T(128)} %pad_add_fusion.me, ...), custom_call_target="tpu_custom_call" | custom-call | flops 805306368 | bytes 4718592 | tf_op jit(solution)/shard_map/pallas_call | solution.py:264
  151.2 2.1 %collective-permute-start.10 = (bf16[24,32,128]{2,1,0:T(8,128)(2,1)}, bf16[24,32,128]{2,1,0:T(8,128)(2,1)S(1)}, u32[]{:S(2)}, u32[]{:S(2)}) collective-permute-start(bf16[24,32,128]{2,1,0:T(8,128)(2,1)} %get-tuple-element.38), channel_id=1, source_target_pairs={{0,2},{2,4},{4,6},{6,1},{1,3},{3,5},{5,7},{7,0},{8,10},{10,12},{12... | collective-permute-start | bytes 589832 | tf_op jit(solution)/shard_map/ppermute | solution.py:392
  153.2 2.4 %collective-permute-start.11 = (bf16[24,32,128]{2,1,0:T(8,128)(2,1)}, bf16[24,32,128]{2,1,0:T(8,128)(2,1)S(1)}, u32[]{:S(2)}, u32[]{:S(2)}) collective-permute-start(bf16[24,32,128]{2,1,0:T(8,128)(2,1)} %get-tuple-element.39), channel_id=1, source_target_pairs={{0,4},{2,6},{4,1},{6,3},{1,5},{3,7},{5,0},{7,2},{8,12},{10,14},{12... | collective-permute-start | bytes 589832 | tf_op jit(solution)/shard_map/ppermute | solution.py:392
  155.6 2.4 %collective-permute-start.12 = (bf16[24,32,128]{2,1,0:T(8,128)(2,1)}, bf16[24,32,128]{2,1,0:T(8,128)(2,1)S(1)}, u32[]{:S(2)}, u32[]{:S(2)}) collective-permute-start(bf16[24,32,128]{2,1,0:T(8,128)(2,1)} %get-tuple-element.40), channel_id=1, source_target_pairs={{0,6},{2,1},{4,3},{6,5},{1,7},{3,0},{5,2},{7,4},{8,14},{10,9},{12,... | collective-permute-start | bytes 589832 | tf_op jit(solution)/shard_map/ppermute | solution.py:392
  160.0 2.9 %collective-permute-done.10.refs_1_ = bf16[24,32,128]{2,1,0:T(8,128)(2,1)S(1)} collective-permute-done((bf16[24,32,128]{2,1,0:T(8,128)(2,1)}, bf16[24,32,128]{2,1,0:T(8,128)(2,1)S(1)}, u32[]{:S(2)}, u32[]{:S(2)}) %collective-permute-start.10) | collective-permute-done | bytes 196640 | tf_op jit(solution)/shard_map/ppermute | solution.py:392
  162.9 10.7 %collective-permute-start.15 = (bf16[24,32,128]{2,1,0:T(8,128)(2,1)}, bf16[24,32,128]{2,1,0:T(8,128)(2,1)S(1)}, u32[]{:S(2)}, u32[]{:S(2)}) collective-permute-start(bf16[24,32,128]{2,1,0:T(8,128)(2,1)} %get-tuple-element.43), channel_id=1, source_target_pairs={{0,5},{2,7},{4,0},{6,2},{1,4},{3,6},{5,1},{7,3},{8,13},{10,15},{12... | collective-permute-start | bytes 589832 | tf_op jit(solution)/shard_map/ppermute | solution.py:392
  173.6 7.7 %collective-permute-done.11.refs_2_ = bf16[24,32,128]{2,1,0:T(8,128)(2,1)S(1)} collective-permute-done((bf16[24,32,128]{2,1,0:T(8,128)(2,1)}, bf16[24,32,128]{2,1,0:T(8,128)(2,1)S(1)}, u32[]{:S(2)}, u32[]{:S(2)}) %collective-permute-start.11) | collective-permute-done | bytes 196640 | tf_op jit(solution)/shard_map/ppermute | solution.py:392
  183.6 5.3 %collective-permute-done.15.refs_6_ = bf16[24,32,128]{2,1,0:T(8,128)(2,1)S(1)} collective-permute-done((bf16[24,32,128]{2,1,0:T(8,128)(2,1)}, bf16[24,32,128]{2,1,0:T(8,128)(2,1)S(1)}, u32[]{:S(2)}, u32[]{:S(2)}) %collective-permute-start.15) | collective-permute-done | bytes 196640 | tf_op jit(solution)/shard_map/ppermute | solution.py:392
  188.9 3.8 %collective-permute-done.16.refs_7_ = bf16[24,32,128]{2,1,0:T(8,128)(2,1)S(1)} collective-permute-done((bf16[24,32,128]{2,1,0:T(8,128)(2,1)}, bf16[24,32,128]{2,1,0:T(8,128)(2,1)S(1)}, u32[]{:S(2)}, u32[]{:S(2)}) %collective-permute-start.16) | collective-permute-done | bytes 196640 | tf_op jit(solution)/shard_map/ppermute | solution.py:392
  193.4 5.0 %shard_map.87 = f32[32,128,256]{2,1,0:T(8,128)} custom-call(s32[3]{0:T(128)} %pad_add_fusion.me, bf16[8,8,32,128]{3,2,1,0:T(8,128)(2,1)} %all-to-all-done.first, bf16[24,32,128]{2,1,0:T(8,128)(2,1)} %get-tuple-element.37.refs_0_, bf16[24,32,128]{2,1,0:T(8,128)(2,1)} %copy-done.2, bf16[24,32,128]{2,1,0:T(8,128)(2,1)} %copy-done.3, ...), custom_call_target="tpu_custom_call" | custom-call | tf_op jit(solution)/shard_map/pallas_call | solution.py:347
  (46 shorter events, 12.4 us)
Async XLA Ops:
  17.9 117.8 %all-to-all-start.1 = ((bf16[32,2,24,1024]{3,2,1,0:T(8,128)(2,1)}), bf16[32,2,24,1024]{3,2,1,0:T(8,128)(2,1)S(1)}, u32[]{:S(2)}, u32[]{:S(2)}) async-start(bf16[32,2,24,1024]{3,2,1,0:T(8,128)(2,1)} %bitcast.12), calls=%async_computation.1 | async-start | bytes 6291456 | tf_op jit(solution)/shard_map/all_to_all | solution.py:375
  34.3 53.5 %collective-permute-start = (bf16[2,4,2,8,1024]{4,3,2,1,0:T(8,128)(2,1)}, bf16[2,4,2,8,1024]{4,3,2,1,0:T(8,128)(2,1)S(1)}, u32[]{:S(2)}, u32[]{:S(2)}) collective-permute-start(bf16[2,4,2,8,1024]{4,3,2,1,0:T(8,128)(2,1)} %get-tuple-element.26), channel_id=1, source_target_pairs={{0,2},{2,4},{4,6},{6,0},{1,3},{3,5},{5,7},{7,1},{8,10},{10,12},{12... | collective-permute-start | bytes 786440 | tf_op jit(solution)/shard_map/ppermute | solution.py:372
  36.1 78.5 %collective-permute-start.1 = (bf16[2,4,2,8,1024]{4,3,2,1,0:T(8,128)(2,1)}, bf16[2,4,2,8,1024]{4,3,2,1,0:T(8,128)(2,1)}, u32[]{:S(2)}, u32[]{:S(2)}) collective-permute-start(bf16[2,4,2,8,1024]{4,3,2,1,0:T(8,128)(2,1)} %get-tuple-element.27), channel_id=1, source_target_pairs={{0,4},{2,6},{4,0},{6,2},{1,5},{3,7},{5,1},{7,3},{8,12},{10,14},{12... | collective-permute-start | bytes 786440 | tf_op jit(solution)/shard_map/ppermute | solution.py:372
  38.5 76.1 %collective-permute-start.2 = (bf16[2,4,2,8,1024]{4,3,2,1,0:T(8,128)(2,1)}, bf16[2,4,2,8,1024]{4,3,2,1,0:T(8,128)(2,1)}, u32[]{:S(2)}, u32[]{:S(2)}) collective-permute-start(bf16[2,4,2,8,1024]{4,3,2,1,0:T(8,128)(2,1)} %get-tuple-element.28), channel_id=1, source_target_pairs={{0,6},{2,0},{4,2},{6,4},{1,7},{3,1},{5,3},{7,5},{8,14},{10,8},{12,... | collective-permute-start | bytes 786440 | tf_op jit(solution)/shard_map/ppermute | solution.py:372
  87.8 26.9 %copy-start.1 = (bf16[2,4,2,8,1024]{4,3,2,1,0:T(8,128)(2,1)}, bf16[2,4,2,8,1024]{4,3,2,1,0:T(8,128)(2,1)S(1)}, u32[]{:S(2)}) copy-start(bf16[2,4,2,8,1024]{4,3,2,1,0:T(8,128)(2,1)S(1)} %collective-permute-done) | copy-start | bytes 786436
  117.1 6.3 %collective-permute-start.3 = (bf16[4,2,8,1024]{3,2,1,0:T(8,128)(2,1)}, bf16[4,2,8,1024]{3,2,1,0:T(8,128)(2,1)S(1)}, u32[]{:S(2)}, u32[]{:S(2)}) collective-permute-start(bf16[4,2,8,1024]{3,2,1,0:T(8,128)(2,1)} %get-tuple-element.30), channel_id=1, source_target_pairs={{0,8},{8,16},{16,24},{24,1},{1,9},{9,17},{17,25},{25,0},{2,10},{10... | collective-permute-start | bytes 393224 | tf_op jit(solution)/shard_map/ppermute | solution.py:380
  117.2 7.6 %collective-permute-start.4 = (bf16[4,2,8,1024]{3,2,1,0:T(8,128)(2,1)}, bf16[4,2,8,1024]{3,2,1,0:T(8,128)(2,1)S(1)}, u32[]{:S(2)}, u32[]{:S(2)}) collective-permute-start(bf16[4,2,8,1024]{3,2,1,0:T(8,128)(2,1)} %get-tuple-element.31), channel_id=1, source_target_pairs={{0,16},{8,24},{16,1},{24,9},{1,17},{9,25},{17,0},{25,8},{2,18},{10... | collective-permute-start | bytes 393224 | tf_op jit(solution)/shard_map/ppermute | solution.py:380
  118.1 8.4 %collective-permute-start.5 = (bf16[4,2,8,1024]{3,2,1,0:T(8,128)(2,1)}, bf16[4,2,8,1024]{3,2,1,0:T(8,128)(2,1)S(1)}, u32[]{:S(2)}, u32[]{:S(2)}) collective-permute-start(bf16[4,2,8,1024]{3,2,1,0:T(8,128)(2,1)} %get-tuple-element.32), channel_id=1, source_target_pairs={{0,24},{8,1},{16,9},{24,17},{1,25},{9,0},{17,8},{25,16},{2,26},{10... | collective-permute-start | bytes 393224 | tf_op jit(solution)/shard_map/ppermute | solution.py:380
  120.4 6.1 %collective-permute-start.6 = (bf16[4,2,8,1024]{3,2,1,0:T(8,128)(2,1)}, bf16[4,2,8,1024]{3,2,1,0:T(8,128)(2,1)}, u32[]{:S(2)}, u32[]{:S(2)}) collective-permute-start(bf16[4,2,8,1024]{3,2,1,0:T(8,128)(2,1)} %get-tuple-element.33), channel_id=1, source_target_pairs={{0,1},{8,9},{16,17},{24,25},{1,0},{9,8},{17,16},{25,24},{2,3},{10,... | collective-permute-start | bytes 393224 | tf_op jit(solution)/shard_map/ppermute | solution.py:380
  121.0 8.3 %collective-permute-start.7 = (bf16[4,2,8,1024]{3,2,1,0:T(8,128)(2,1)}, bf16[4,2,8,1024]{3,2,1,0:T(8,128)(2,1)}, u32[]{:S(2)}, u32[]{:S(2)}) collective-permute-start(bf16[4,2,8,1024]{3,2,1,0:T(8,128)(2,1)} %get-tuple-element.34), channel_id=1, source_target_pairs={{0,9},{8,17},{16,25},{24,0},{1,8},{9,16},{17,24},{25,1},{2,11},{10... | collective-permute-start | bytes 393224 | tf_op jit(solution)/shard_map/ppermute | solution.py:380
  123.4 6.9 %collective-permute-start.8 = (bf16[4,2,8,1024]{3,2,1,0:T(8,128)(2,1)}, bf16[4,2,8,1024]{3,2,1,0:T(8,128)(2,1)}, u32[]{:S(2)}, u32[]{:S(2)}) collective-permute-start(bf16[4,2,8,1024]{3,2,1,0:T(8,128)(2,1)} %get-tuple-element.35), channel_id=1, source_target_pairs={{0,17},{8,25},{16,0},{24,8},{1,16},{9,24},{17,1},{25,9},{2,19},{10... | collective-permute-start | bytes 393224 | tf_op jit(solution)/shard_map/ppermute | solution.py:380
  124.8 6.9 %collective-permute-start.9 = (bf16[4,2,8,1024]{3,2,1,0:T(8,128)(2,1)}, bf16[4,2,8,1024]{3,2,1,0:T(8,128)(2,1)}, u32[]{:S(2)}, u32[]{:S(2)}) collective-permute-start(bf16[4,2,8,1024]{3,2,1,0:T(8,128)(2,1)} %get-tuple-element.36), channel_id=1, source_target_pairs={{0,25},{8,0},{16,8},{24,16},{1,24},{9,1},{17,9},{25,17},{2,27},{10... | collective-permute-start | bytes 393224 | tf_op jit(solution)/shard_map/ppermute | solution.py:380
  135.8 47.8 %all-to-all-start = ((bf16[8,8,32,128]{3,2,1,0:T(8,128)(2,1)}), bf16[8,8,32,128]{3,2,1,0:T(8,128)(2,1)}, u32[]{:S(2)}, u32[]{:S(2)}) async-start(bf16[8,8,32,128]{3,2,1,0:T(8,128)(2,1)} %shard_map.84), calls=%async_computation | async-start | bytes 1048576 | tf_op jit(solution)/shard_map/all_to_all | solution.py:387
  151.2 11.7 %collective-permute-start.10 = (bf16[24,32,128]{2,1,0:T(8,128)(2,1)}, bf16[24,32,128]{2,1,0:T(8,128)(2,1)S(1)}, u32[]{:S(2)}, u32[]{:S(2)}) collective-permute-start(bf16[24,32,128]{2,1,0:T(8,128)(2,1)} %get-tuple-element.38), channel_id=1, source_target_pairs={{0,2},{2,4},{4,6},{6,1},{1,3},{3,5},{5,7},{7,0},{8,10},{10,12},{12... | collective-permute-start | bytes 589832 | tf_op jit(solution)/shard_map/ppermute | solution.py:392
  153.2 28.1 %collective-permute-start.11 = (bf16[24,32,128]{2,1,0:T(8,128)(2,1)}, bf16[24,32,128]{2,1,0:T(8,128)(2,1)S(1)}, u32[]{:S(2)}, u32[]{:S(2)}) collective-permute-start(bf16[24,32,128]{2,1,0:T(8,128)(2,1)} %get-tuple-element.39), channel_id=1, source_target_pairs={{0,4},{2,6},{4,1},{6,3},{1,5},{3,7},{5,0},{7,2},{8,12},{10,14},{12... | collective-permute-start | bytes 589832 | tf_op jit(solution)/shard_map/ppermute | solution.py:392
  155.6 28.0 %collective-permute-start.12 = (bf16[24,32,128]{2,1,0:T(8,128)(2,1)}, bf16[24,32,128]{2,1,0:T(8,128)(2,1)S(1)}, u32[]{:S(2)}, u32[]{:S(2)}) collective-permute-start(bf16[24,32,128]{2,1,0:T(8,128)(2,1)} %get-tuple-element.40), channel_id=1, source_target_pairs={{0,6},{2,1},{4,3},{6,5},{1,7},{3,0},{5,2},{7,4},{8,14},{10,9},{12,... | collective-permute-start | bytes 589832 | tf_op jit(solution)/shard_map/ppermute | solution.py:392
  158.0 25.6 %collective-permute-start.13 = (bf16[24,32,128]{2,1,0:T(8,128)(2,1)}, bf16[24,32,128]{2,1,0:T(8,128)(2,1)S(1)}, u32[]{:S(2)}, u32[]{:S(2)}) collective-permute-start(bf16[24,32,128]{2,1,0:T(8,128)(2,1)} %get-tuple-element.41), channel_id=1, source_target_pairs={{0,1},{2,3},{4,5},{6,7},{1,0},{3,2},{5,4},{7,6},{8,9},{10,11},{12,... | collective-permute-start | bytes 589832 | tf_op jit(solution)/shard_map/ppermute | solution.py:392
  158.5 25.1 %collective-permute-start.14 = (bf16[24,32,128]{2,1,0:T(8,128)(2,1)}, bf16[24,32,128]{2,1,0:T(8,128)(2,1)S(1)}, u32[]{:S(2)}, u32[]{:S(2)}) collective-permute-start(bf16[24,32,128]{2,1,0:T(8,128)(2,1)} %get-tuple-element.42), channel_id=1, source_target_pairs={{0,3},{2,5},{4,7},{6,0},{1,2},{3,4},{5,6},{7,1},{8,11},{10,13},{12... | collective-permute-start | bytes 589832 | tf_op jit(solution)/shard_map/ppermute | solution.py:392
  162.9 29.8 %copy-start.2 = (bf16[24,32,128]{2,1,0:T(8,128)(2,1)}, bf16[24,32,128]{2,1,0:T(8,128)(2,1)S(1)}, u32[]{:S(2)}) copy-start(bf16[24,32,128]{2,1,0:T(8,128)(2,1)S(1)} %collective-permute-done.10.refs_1_) | copy-start | bytes 589828
  162.9 26.0 %collective-permute-start.15 = (bf16[24,32,128]{2,1,0:T(8,128)(2,1)}, bf16[24,32,128]{2,1,0:T(8,128)(2,1)S(1)}, u32[]{:S(2)}, u32[]{:S(2)}) collective-permute-start(bf16[24,32,128]{2,1,0:T(8,128)(2,1)} %get-tuple-element.43), channel_id=1, source_target_pairs={{0,5},{2,7},{4,0},{6,2},{1,4},{3,6},{5,1},{7,3},{8,13},{10,15},{12... | collective-permute-start | bytes 589832 | tf_op jit(solution)/shard_map/ppermute | solution.py:392
  181.3 11.4 %copy-start.3 = (bf16[24,32,128]{2,1,0:T(8,128)(2,1)}, bf16[24,32,128]{2,1,0:T(8,128)(2,1)S(1)}, u32[]{:S(2)}) copy-start(bf16[24,32,128]{2,1,0:T(8,128)(2,1)S(1)} %collective-permute-done.11.refs_2_) | copy-start | bytes 589828
  181.3 11.4 %collective-permute-start.16 = (bf16[24,32,128]{2,1,0:T(8,128)(2,1)}, bf16[24,32,128]{2,1,0:T(8,128)(2,1)S(1)}, u32[]{:S(2)}, u32[]{:S(2)}) collective-permute-start(bf16[24,32,128]{2,1,0:T(8,128)(2,1)} %get-tuple-element.44), channel_id=1, source_target_pairs={{0,7},{2,0},{4,2},{6,4},{1,6},{3,1},{5,3},{7,5},{8,15},{10,8},{12,... | collective-permute-start | bytes 589832 | tf_op jit(solution)/shard_map/ppermute | solution.py:392
  183.6 9.2 %copy-start.4 = (bf16[24,32,128]{2,1,0:T(8,128)(2,1)}, bf16[24,32,128]{2,1,0:T(8,128)(2,1)S(1)}, u32[]{:S(2)}) copy-start(bf16[24,32,128]{2,1,0:T(8,128)(2,1)S(1)} %collective-permute-done.12.refs_3_) | copy-start | bytes 589828
  183.6 9.2 %copy-start.5 = (bf16[24,32,128]{2,1,0:T(8,128)(2,1)}, bf16[24,32,128]{2,1,0:T(8,128)(2,1)S(1)}, u32[]{:S(2)}) copy-start(bf16[24,32,128]{2,1,0:T(8,128)(2,1)S(1)} %collective-permute-done.13.refs_4_) | copy-start | bytes 589828
  (7 other events, 41.7 us)
where the time goes:
time: 199 us
  waiting for transfers between devices  102 us (51%)
  starting transfers between devices  48.6 us (24%)
  Pallas kernels  45.4 us (23%)
    ppermute x3, waiting for transfers between devices, shards(): lax.ppermute(blocks[k], 'row', [(x, (x + k) % rows) for x in range(rows)])  74.7 us
    pallas_call x2, Pallas kernels, dft(): pl.pallas_call(functools.partial(dft_kernel, kinds, rows_apart), in_specs...  26.3 us
    ppermute x7, starting transfers between devices, shards(): pieces[k] = lax.ppermute(pieces[k], OWNERS[::-1], pairs)  21.2 us
    ppermute x7, waiting for transfers between devices, shards(): pieces[k] = lax.ppermute(pieces[k], OWNERS[::-1], pairs)  19.7 us
    pallas_call x2, Pallas kernels, correlate(): pl.pallas_call(functools.partial(correlate_kernel, sizes, count), in_spec...  11.7 us
    ppermute x7, waiting for transfers between devices, shards(): blocks[q] = lax.ppermute(blocks[q], ('freq', 'col'), pairs)  7.9 us
    all_to_all x1, starting transfers between devices, shards(): lax.all_to_all(first, OWNERS, split_axis=0, concat_axis=0, tiled=True)  7.81 us
    all_to_all x1, starting transfers between devices, shards(): lax.all_to_all(sent, EVERYONE, split_axis=0, concat_axis=0, tiled=True)  7.32 us
  transfers between devices with their start and end apart: 19, of which 11 were waited for; matrix products, arithmetic and copies ran while one was open for 0% of the time, Pallas kernels for 12%

commit v1 on v0

--- a/solution.py
+++ b/solution.py
@@ -17,10 +17,32 @@
 ANYWHERE = pl.BlockSpec(memory_space=pl.ANY)
 SCALARS = pl.BlockSpec(memory_space=pltpu.SMEM)
 
-FOURS = (0, 4, ((1, 1, 1, 1),))
-TWOS = (2, 4, ((1, -1, 1, -1),))
-ODDS = (1, 2, ((1, 0, -1, 0), (0, 1, 0, -1)))
-CHUNKS = ((FOURS,), (TWOS, ODDS))
+ROOT = math.sqrt(0.5)
+
+
+def fours(x):
+    return [(x[0] + x[4]) + (x[2] + x[6]), (x[1] + x[5]) + (x[3] + x[7])]
+
+
+def twos(x):
+    return [(x[0] + x[4]) - (x[2] + x[6]), (x[1] + x[5]) - (x[3] + x[7])]
+
+
+def ones(x):
+    turned = ((x[1] - x[5]) - (x[3] - x[7])) * ROOT, ((x[1] - x[5]) + (x[3] - x[7])) * ROOT
+    return [(x[0] - x[4]) + turned[0], -(x[2] - x[6]) - turned[1]]
+
+
+def fives(x):
+    turned = ((x[1] - x[5]) - (x[3] - x[7])) * ROOT, ((x[1] - x[5]) + (x[3] - x[7])) * ROOT
+    return [(x[0] - x[4]) - turned[0], turned[1] - (x[2] - x[6])]
+
+
+FOURS = (4, {0: 0}, fours)
+TWOS = (4, {2: 0}, twos)
+ONES = (8, {1: 1, 7: -1}, ones)
+FIVES = (8, {3: -1, 5: 1}, fives)
+CHUNKS = ((FOURS,), (TWOS, ONES, FIVES))
 PAD = 8
 
 
@@ -30,24 +52,23 @@
     return high, low
 
 
+def places(kind, total):
+    modulus, residues, _ = kind
+    return [x for x in range(total) if x % modulus in residues]
+
+
 def angle_tables(length, channels, kind):
-    residue, modulus, folds = kind
+    modulus, residues, _ = kind
     stride = 2 ** ((channels.bit_length() - 1) // 2)
-    sample = np.arange(length // 4 * len(folds))
+    fine = np.array(places(kind, stride))
+    signs = np.array([residues[x % modulus] for x in fine])
+    sample = np.arange(length // 8 if signs.any() else length // 4)
     factor = 1.0 / (64.0 * math.sqrt(length))
     coarse = 2.0 * math.pi / length * ((np.arange(0, channels, stride)[:, None] * sample) % length)
-    fine = 2.0 * math.pi / length * ((np.arange(residue, stride, modulus)[:, None] * sample) % length)
+    fine = 2.0 * math.pi / length * ((fine[:, None] * sample) % length)
     coarse = np.stack([np.cos(coarse), np.sin(coarse)]) * factor
-    fine = np.stack([np.cos(fine), np.sin(fine)])
+    fine = np.stack([np.cos(fine), np.sin(fine), np.broadcast_to(signs[:, None], fine.shape)])
     return jnp.asarray(coarse, jnp.float32), jnp.asarray(fine, jnp.float32)
-
-
-def signed_sum(values, signs):
-    total = None
-    for value, sign in zip(values, signs):
-        if sign:
-            total = value * sign if total is None else (total + value if sign > 0 else total - value)
-    return total
 
 
 def dft_kernel(kinds, rows_apart, me, source, taps, *refs):
@@ -55,11 +76,11 @@
     out, volts, sem, fold = scratch[len(outs) : len(outs) + 4]
     scratch = scratch[len(outs) + 4 :]
     frames, inputs, length = volts.shape
-    quarter = length // 4
+    eighth = length // 8
     tap_count = taps.shape[0]
     spec_count = frames - tap_count + 1
     step, lanes, stages = 16, 128, sem.shape[0]
-    rows, tiles = step * inputs, quarter // lanes
+    rows, tiles = step * inputs, eighth // lanes
     bounds = [spec_count * x // stages + (tap_count - 1 if x else 0) for x in range(stages + 1)]
     copies = []
     for x in range(stages):
@@ -70,8 +91,8 @@
     def filter_rows(index, carry):
         for tile in range(tiles):
             values = []
-            for x in range(4):
-                at = pl.ds(x * quarter + tile * lanes, lanes)
+            for x in range(8):
+                at = pl.ds(x * eighth + tile * lanes, lanes)
                 weight = taps[:, at].astype(jnp.float32) / 4096.0
                 block = volts[pl.ds(index * step, step + tap_count - 1), :, at].astype(jnp.float32).reshape(-1, lanes)
                 value = weight[0:1] * block[:rows]
@@ -79,10 +100,9 @@
                     value = value + weight[k : k + 1] * block[k * inputs : k * inputs + rows]
                 values.append(value)
             piece = 0
-            for _, _, folds in kinds:
-                for signs in folds:
-                    at = pl.ds(pl.multiple_of(index * rows, rows), rows)
-                    fold[piece * tiles + tile, at, :] = signed_sum(values, signs)
+            for _, _, folded in kinds:
+                for value in folded(values):
+                    fold[piece * tiles + tile, pl.ds(pl.multiple_of(index * rows, rows), rows), :] = value
                     piece += 1
         return carry
 
@@ -90,12 +110,12 @@
         copies[x].wait()
         lax.fori_loop(spec_count * x // stages // step, spec_count * (x + 1) // stages // step, filter_rows, 0)
     piece = 0
-    for x, (_, _, folds) in enumerate(kinds):
+    for x in range(len(kinds)):
         high, low = scratch[4 * x : 4 * x + 2]
-        for y in range(len(folds)):
+        for y in range(2):
             for tile in range(tiles):
                 for i in range(inputs):
-                    at = pl.ds(i * spec_count, spec_count), pl.ds(y * quarter + tile * lanes, lanes)
+                    at = pl.ds(i * spec_count, spec_count), pl.ds(y * eighth + tile * lanes, lanes)
                     high[at], low[at] = split(fold[piece, pl.ds(i, spec_count, stride=inputs), :])
                 piece += 1
 
@@ -109,11 +129,15 @@
         fine_count = fine.shape[1]
         for a in range(channels // fine_count):
             cos_a, sin_a = coarse[0, a : a + 1], coarse[1, a : a + 1]
-            real = cos_a * fine[0] - sin_a * fine[1]
-            imag = -(sin_a * fine[0]) - cos_a * fine[1]
-            for part, value in enumerate((real, imag)):
-                at = pl.ds(part * channels + a * fine_count, fine_count)
-                table_high[at], table_low[at] = split(value)
+            cosine = cos_a * fine[0] - sin_a * fine[1]
+            sine = sin_a * fine[0] + cos_a * fine[1]
+            values = [(cosine, -sine)]
+            if cosine.shape[1] < table_high.shape[1]:
+                values.append((sine * fine[2], cosine * fine[2]))
+            for y, pair in enumerate(values):
+                for part, value in enumerate(pair):
+                    at = pl.ds(part * channels + a * fine_count, fine_count), pl.ds(y * eighth, value.shape[1])
+                    table_high[at], table_low[at] = split(value)
         result = dot(table_high[...], high[...]) + (dot(table_high[...], low[...]) + dot(table_low[...], high[...]))
         result = result.astype(jnp.bfloat16)
         each = channels // groups // owners
@@ -144,12 +168,11 @@
     channels = length // 2
     operands, scratch, count, pieces, flops = [me, volts, taps], [], 0, 0, 0
     for kind in kinds:
-        _, modulus, folds = kind
         operands += angle_tables(length, channels, kind)
-        folded, rows = length // 4 * len(folds), 2 * channels // modulus
+        folded, rows = length // 4, 2 * len(places(kind, channels))
         scratch += [pltpu.VMEM((width, folded), jnp.bfloat16)] * 2 + [pltpu.VMEM((rows, folded), jnp.bfloat16)] * 2
-        count += channels // modulus // groups // owners
-        pieces += len(folds)
+        count += rows // 2 // groups // owners
+        pieces += 2
         flops += 6 * rows * folded * width
     shape = (owners, groups, 2, count, width)
     out_shape = jax.ShapeDtypeStruct((owners // (rows_apart or 1),) + shape[1:] if rows_apart else shape, jnp.bfloat16)
@@ -162,7 +185,7 @@
             pltpu.VMEM(shape, jnp.bfloat16),
             pltpu.VMEM(volts.shape, volts.dtype),
             pltpu.SemaphoreType.DMA((4, owners)),
-            pltpu.VMEM((pieces * (length // 4 // 128), width, 128), jnp.float32),
+            pltpu.VMEM((pieces * (length // 8 // 128), width, 128), jnp.float32),
             *scratch,
         ],
         cost_estimate=pl.CostEstimate(
@@ -279,13 +302,6 @@
     )(me, *got)
 
 
-def places(count_of):
-    result = []
-    for kinds in CHUNKS:
-        result.append([residue + modulus * x for residue, modulus, _ in kinds for x in range(count_of(modulus))])
-    return result
-
-
 def finish_kernel(sizes, me, first, *refs):
     pieces, (same, out, scratch, held, sem) = refs[:-5], refs[-5:]
     cols, rows, groups, inputs = sizes
@@ -295,7 +311,7 @@
     pitch = scratch.shape[1] // (owners * total)
     whole = [(k, first.at[k], 0) for k in range(owners)]
     whole += [(lax.rem(me[0] + (owners - k), owners), piece, 1) for k, piece in enumerate(pieces)]
-    slots_of = places(lambda modulus: total // modulus)
+    slots_of = [sum((places(kind, total) for kind in kinds), []) for kinds in CHUNKS]
     for owner, got, chunk in whole:
         for slot, place in enumerate(slots_of[chunk]):
             for tile in range(tiles):
@@ -339,7 +355,7 @@
     total = first.shape[1] + pieces[0].shape[0]
     channels = owners * total
     if channels % 128 or 128 % (rows * groups):
-        order = np.argsort(sum(places(lambda modulus: total // modulus), []))
+        order = np.argsort(sum((places(kind, total) for kinds in CHUNKS for kind in kinds), []))
         second = jnp.stack(pieces)[(me[0] - jnp.arange(owners)) % owners]
         value = jnp.concatenate([first, second], axis=1)[:, order]
         value = value.reshape(channels, inputs, cols, groups, 2, inputs, rows, groups)

time: 199 us -> 195 us (0.980)
  Pallas kernels: 45.4 us -> 41.9 us
    pallas_call x2, Pallas kernels: 26.3 us -> 22.7 us  [dft(): pl.pallas_call(functools.partial(dft_kernel, kinds, rows_apart), in_specs...]
where the time goes in v1:
time: 195 us
  waiting for transfers between devices  102 us (52%)
  starting transfers between devices  48.6 us (25%)
  Pallas kernels  41.9 us (21%)
    ppermute x3, waiting for transfers between devices, shards(): lax.ppermute(blocks[k], 'row', [(x, (x + k) % rows) for x in range(rows)])  74.7 us
    pallas_call x2, Pallas kernels, dft(): pl.pallas_call(functools.partial(dft_kernel, kinds, rows_apart), in_specs...  22.7 us
    ppermute x7, starting transfers between devices, shards(): pieces[k] = lax.ppermute(pieces[k], OWNERS[::-1], pairs)  21.2 us
    ppermute x7, waiting for transfers between devices, shards(): pieces[k] = lax.ppermute(pieces[k], OWNERS[::-1], pairs)  19.7 us
    pallas_call x2, Pallas kernels, correlate(): pl.pallas_call(functools.partial(correlate_kernel, sizes, count), in_spec...  11.7 us
    ppermute x7, waiting for transfers between devices, shards(): blocks[q] = lax.ppermute(blocks[q], ('freq', 'col'), pairs)  7.9 us
    all_to_all x1, starting transfers between devices, shards(): lax.all_to_all(first, OWNERS, split_axis=0, concat_axis=0, tiled=True)  7.81 us
    all_to_all x1, starting transfers between devices, shards(): lax.all_to_all(sent, EVERYONE, split_axis=0, concat_axis=0, tiled=True)  7.33 us
  transfers between devices with their start and end apart: 19, of which 11 were waited for; matrix products, arithmetic and copies ran while one was open for 0% of the time, Pallas kernels for 12%

profile of v1, /device:TPU:0, one launch (start us, length us, event | category | flops | bytes accessed | tf_op | source)
XLA Modules:
  0.0 194.9 jit_solution(1265520926791613136)
XLA Ops:
  0.7 13.7 %shard_map.103 = bf16[8,4,2,24,1024]{4,3,2,1,0:T(8,128)(2,1)} custom-call(s32[3]{0:T(128)} %pad_add_fusion.me, bf16[259,4,2048]{2,1,0:T(4,128)(2,1)} %bitcast.15, s32[4,2048]{1,0:T(4,128)} %taps.3, f32[2,32,512]{2,1,0:T(8,128)} %constant.25.clone.refs_0_, f32[3,8,512]{2,1,0:T(8,128)} %constant.27.clone.refs_1_, ...), custom_call_target="tpu_custom_call" | custom-call | flops 4831838208 | bytes 7389184 | tf_op jit(solution)/shard_map/pallas_call | solution.py:179
  14.3 7.3 %all-to-all-start.1 = ((bf16[32,2,24,1024]{3,2,1,0:T(8,128)(2,1)}), bf16[32,2,24,1024]{3,2,1,0:T(8,128)(2,1)S(1)}, u32[]{:S(2)}, u32[]{:S(2)}) async-start(bf16[32,2,24,1024]{3,2,1,0:T(8,128)(2,1)} %bitcast.12), calls=%async_computation.1 | async-start | bytes 6291456 | tf_op jit(solution)/shard_map/all_to_all | solution.py:391
  21.7 9.1 %shard_map.100 = (bf16[2,4,2,8,1024]{4,3,2,1,0:T(8,128)(2,1)}, bf16[2,4,2,8,1024]{4,3,2,1,0:T(8,128)(2,1)}, bf16[2,4,2,8,1024]{4,3,2,1,0:T(8,128)(2,1)}, bf16[2,4,2,8,1024]{4,3,2,1,0:T(8,128)(2,1)}) custom-call(s32[3]{0:T(128)} %pad_add_fusion.me, bf16[259,4,2048]{2,1,0:T(4,128)(2,1)} %bitcast.16, s32[4,2048]{1,0:T(4,128)} %taps.3, ...), custom_call_target="tpu_custom_call" | custom-call | flops 1610612736 | bytes 5292032 | tf_op jit(solution)/shard_map/pallas_call | solution.py:179
  30.7 1.8 collective-permute-start
  32.6 2.4 %collective-permute-start.1 = (bf16[2,4,2,8,1024]{4,3,2,1,0:T(8,128)(2,1)}, bf16[2,4,2,8,1024]{4,3,2,1,0:T(8,128)(2,1)}, u32[]{:S(2)}, u32[]{:S(2)}) collective-permute-start(bf16[2,4,2,8,1024]{4,3,2,1,0:T(8,128)(2,1)} %get-tuple-element.27), channel_id=1, source_target_pairs={{0,4},{2,6},{4,0},{6,2},{1,5},{3,7},{5,1},{7,3},{8,12},{10,14},{12... | collective-permute-start | bytes 786440 | tf_op jit(solution)/shard_map/ppermute | solution.py:388
  36.4 47.8 %collective-permute-done = bf16[2,4,2,8,1024]{4,3,2,1,0:T(8,128)(2,1)S(1)} collective-permute-done((bf16[2,4,2,8,1024]{4,3,2,1,0:T(8,128)(2,1)}, bf16[2,4,2,8,1024]{4,3,2,1,0:T(8,128)(2,1)S(1)}, u32[]{:S(2)}, u32[]{:S(2)}) %collective-permute-start) | collective-permute-done | bytes 262176 | tf_op jit(solution)/shard_map/ppermute | solution.py:388
  84.2 26.9 %collective-permute-done.1 = bf16[2,4,2,8,1024]{4,3,2,1,0:T(8,128)(2,1)} collective-permute-done((bf16[2,4,2,8,1024]{4,3,2,1,0:T(8,128)(2,1)}, bf16[2,4,2,8,1024]{4,3,2,1,0:T(8,128)(2,1)}, u32[]{:S(2)}, u32[]{:S(2)}) %collective-permute-start.1) | collective-permute-done | bytes 262176 | tf_op jit(solution)/shard_map/ppermute | solution.py:388
  111.1 2.5 %shard_map.101 = (bf16[4,2,8,1024]{3,2,1,0:T(8,128)(2,1)}, bf16[4,2,8,1024]{3,2,1,0:T(8,128)(2,1)}, bf16[4,2,8,1024]{3,2,1,0:T(8,128)(2,1)}, bf16[4,2,8,1024]{3,...) custom-call(s32[3]{0:T(128)} %pad_add_fusion.me, ...), custom_call_target="tpu_custom_call" | custom-call | tf_op jit(solution)/shard_map/pallas_call | solution.py:216
  114.6 2.3 %collective-permute-start.5 = (bf16[4,2,8,1024]{3,2,1,0:T(8,128)(2,1)}, bf16[4,2,8,1024]{3,2,1,0:T(8,128)(2,1)S(1)}, u32[]{:S(2)}, u32[]{:S(2)}) collective-permute-start(bf16[4,2,8,1024]{3,2,1,0:T(8,128)(2,1)} %get-tuple-element.32), channel_id=1, source_target_pairs={{0,24},{8,1},{16,9},{24,17},{1,25},{9,0},{17,8},{25,16},{2,26},{10... | collective-permute-start | bytes 393224 | tf_op jit(solution)/shard_map/ppermute | solution.py:396
  117.5 2.4 %collective-permute-done.3.refs_1_ = bf16[4,2,8,1024]{3,2,1,0:T(8,128)(2,1)S(1)} collective-permute-done((bf16[4,2,8,1024]{3,2,1,0:T(8,128)(2,1)}, bf16[4,2,8,1024]{3,2,1,0:T(8,128)(2,1)S(1)}, u32[]{:S(2)}, u32[]{:S(2)}) %collective-permute-start.3) | collective-permute-done | bytes 131104 | tf_op jit(solution)/shard_map/ppermute | solution.py:396
  121.2 1.8 collective-permute-start.9
  123.0 2.7 %collective-permute-done.7.refs_5_ = bf16[4,2,8,1024]{3,2,1,0:T(8,128)(2,1)} collective-permute-done((bf16[4,2,8,1024]{3,2,1,0:T(8,128)(2,1)}, bf16[4,2,8,1024]{3,2,1,0:T(8,128)(2,1)}, u32[]{:S(2)}, u32[]{:S(2)}) %collective-permute-start.7) | collective-permute-done | bytes 131104 | tf_op jit(solution)/shard_map/ppermute | solution.py:396
  128.1 4.1 %shard_map.102 = bf16[8,8,32,128]{3,2,1,0:T(8,128)(2,1)} custom-call(s32[3]{0:T(128)} %pad_add_fusion.me, bf16[4,2,8,1024]{3,2,1,0:T(8,128)(2,1)} %get-tuple-element.29.refs_0_, bf16[4,2,8,1024]{3,2,1,0:T(8,128)(2,1)} %copy-done.9, bf16[4,2,8,1024]{3,2,1,0:T(8,128)(2,1)} %copy-done.10, bf16[4,2,8,1024]{3,2,1,0:T(8,128)(2,1)} %copy-done.11, ...), custom_call_target="tpu_custom_call" | custom-call | flops 268435456 | bytes 1572864 | tf_op jit(solution)/shard_map/pallas_call | solution.py:287
  132.2 7.8 %all-to-all-start = ((bf16[8,8,32,128]{3,2,1,0:T(8,128)(2,1)}), bf16[8,8,32,128]{3,2,1,0:T(8,128)(2,1)}, u32[]{:S(2)}, u32[]{:S(2)}) async-start(bf16[8,8,32,128]{3,2,1,0:T(8,128)(2,1)} %shard_map.102), calls=%async_computation | async-start | bytes 1048576 | tf_op jit(solution)/shard_map/all_to_all | solution.py:403
  140.0 7.6 %shard_map.104 = (bf16[24,32,128]{2,1,0:T(8,128)(2,1)}, bf16[24,32,128]{2,1,0:T(8,128)(2,1)}, bf16[24,32,128]{2,1,0:T(8,128)(2,1)}, bf16[24,32,128]{2,1,0:T(8,12...) custom-call(s32[3]{0:T(128)} %pad_add_fusion.me, ...), custom_call_target="tpu_custom_call" | custom-call | flops 805306368 | bytes 4718592 | tf_op jit(solution)/shard_map/pallas_call | solution.py:287
  147.6 2.1 %collective-permute-start.10 = (bf16[24,32,128]{2,1,0:T(8,128)(2,1)}, bf16[24,32,128]{2,1,0:T(8,128)(2,1)S(1)}, u32[]{:S(2)}, u32[]{:S(2)}) collective-permute-start(bf16[24,32,128]{2,1,0:T(8,128)(2,1)} %get-tuple-element.38), channel_id=1, source_target_pairs={{0,2},{2,4},{4,6},{6,1},{1,3},{3,5},{5,7},{7,0},{8,10},{10,12},{12... | collective-permute-start | bytes 589832 | tf_op jit(solution)/shard_map/ppermute | solution.py:408
  149.7 2.4 %collective-permute-start.11 = (bf16[24,32,128]{2,1,0:T(8,128)(2,1)}, bf16[24,32,128]{2,1,0:T(8,128)(2,1)S(1)}, u32[]{:S(2)}, u32[]{:S(2)}) collective-permute-start(bf16[24,32,128]{2,1,0:T(8,128)(2,1)} %get-tuple-element.39), channel_id=1, source_target_pairs={{0,4},{2,6},{4,1},{6,3},{1,5},{3,7},{5,0},{7,2},{8,12},{10,14},{12... | collective-permute-start | bytes 589832 | tf_op jit(solution)/shard_map/ppermute | solution.py:408
  152.0 2.4 %collective-permute-start.12 = (bf16[24,32,128]{2,1,0:T(8,128)(2,1)}, bf16[24,32,128]{2,1,0:T(8,128)(2,1)S(1)}, u32[]{:S(2)}, u32[]{:S(2)}) collective-permute-start(bf16[24,32,128]{2,1,0:T(8,128)(2,1)} %get-tuple-element.40), channel_id=1, source_target_pairs={{0,6},{2,1},{4,3},{6,5},{1,7},{3,0},{5,2},{7,4},{8,14},{10,9},{12,... | collective-permute-start | bytes 589832 | tf_op jit(solution)/shard_map/ppermute | solution.py:408
  156.4 2.9 %collective-permute-done.10.refs_1_ = bf16[24,32,128]{2,1,0:T(8,128)(2,1)S(1)} collective-permute-done((bf16[24,32,128]{2,1,0:T(8,128)(2,1)}, bf16[24,32,128]{2,1,0:T(8,128)(2,1)S(1)}, u32[]{:S(2)}, u32[]{:S(2)}) %collective-permute-start.10) | collective-permute-done | bytes 196640 | tf_op jit(solution)/shard_map/ppermute | solution.py:408
  159.3 10.7 %collective-permute-start.15 = (bf16[24,32,128]{2,1,0:T(8,128)(2,1)}, bf16[24,32,128]{2,1,0:T(8,128)(2,1)S(1)}, u32[]{:S(2)}, u32[]{:S(2)}) collective-permute-start(bf16[24,32,128]{2,1,0:T(8,128)(2,1)} %get-tuple-element.43), channel_id=1, source_target_pairs={{0,5},{2,7},{4,0},{6,2},{1,4},{3,6},{5,1},{7,3},{8,13},{10,15},{12... | collective-permute-start | bytes 589832 | tf_op jit(solution)/shard_map/ppermute | solution.py:408
  170.0 7.7 %collective-permute-done.11.refs_2_ = bf16[24,32,128]{2,1,0:T(8,128)(2,1)S(1)} collective-permute-done((bf16[24,32,128]{2,1,0:T(8,128)(2,1)}, bf16[24,32,128]{2,1,0:T(8,128)(2,1)S(1)}, u32[]{:S(2)}, u32[]{:S(2)}) %collective-permute-start.11) | collective-permute-done | bytes 196640 | tf_op jit(solution)/shard_map/ppermute | solution.py:408
  180.0 5.3 %collective-permute-done.15.refs_6_ = bf16[24,32,128]{2,1,0:T(8,128)(2,1)S(1)} collective-permute-done((bf16[24,32,128]{2,1,0:T(8,128)(2,1)}, bf16[24,32,128]{2,1,0:T(8,128)(2,1)S(1)}, u32[]{:S(2)}, u32[]{:S(2)}) %collective-permute-start.15) | collective-permute-done | bytes 196640 | tf_op jit(solution)/shard_map/ppermute | solution.py:408
  185.4 3.8 %collective-permute-done.16.refs_7_ = bf16[24,32,128]{2,1,0:T(8,128)(2,1)S(1)} collective-permute-done((bf16[24,32,128]{2,1,0:T(8,128)(2,1)}, bf16[24,32,128]{2,1,0:T(8,128)(2,1)S(1)}, u32[]{:S(2)}, u32[]{:S(2)}) %collective-permute-start.16) | collective-permute-done | bytes 196640 | tf_op jit(solution)/shard_map/ppermute | solution.py:408
  189.8 5.0 %shard_map.105 = f32[32,128,256]{2,1,0:T(8,128)} custom-call(s32[3]{0:T(128)} %pad_add_fusion.me, bf16[8,8,32,128]{3,2,1,0:T(8,128)(2,1)} %all-to-all-done.first, bf16[24,32,128]{2,1,0:T(8,128)(2,1)} %get-tuple-element.37.refs_0_, bf16[24,32,128]{2,1,0:T(8,128)(2,1)} %copy-done.2, bf16[24,32,128]{2,1,0:T(8,128)(2,1)} %copy-done.3, ...), custom_call_target="tpu_custom_call" | custom-call | tf_op jit(solution)/shard_map/pallas_call | solution.py:363
  (46 shorter events, 12.4 us)
Async XLA Ops:
  14.3 117.8 %all-to-all-start.1 = ((bf16[32,2,24,1024]{3,2,1,0:T(8,128)(2,1)}), bf16[32,2,24,1024]{3,2,1,0:T(8,128)(2,1)S(1)}, u32[]{:S(2)}, u32[]{:S(2)}) async-start(bf16[32,2,24,1024]{3,2,1,0:T(8,128)(2,1)} %bitcast.12), calls=%async_computation.1 | async-start | bytes 6291456 | tf_op jit(solution)/shard_map/all_to_all | solution.py:391
  30.7 53.5 %collective-permute-start = (bf16[2,4,2,8,1024]{4,3,2,1,0:T(8,128)(2,1)}, bf16[2,4,2,8,1024]{4,3,2,1,0:T(8,128)(2,1)S(1)}, u32[]{:S(2)}, u32[]{:S(2)}) collective-permute-start(bf16[2,4,2,8,1024]{4,3,2,1,0:T(8,128)(2,1)} %get-tuple-element.26), channel_id=1, source_target_pairs={{0,2},{2,4},{4,6},{6,0},{1,3},{3,5},{5,7},{7,1},{8,10},{10,12},{12... | collective-permute-start | bytes 786440 | tf_op jit(solution)/shard_map/ppermute | solution.py:388
  32.6 78.5 %collective-permute-start.1 = (bf16[2,4,2,8,1024]{4,3,2,1,0:T(8,128)(2,1)}, bf16[2,4,2,8,1024]{4,3,2,1,0:T(8,128)(2,1)}, u32[]{:S(2)}, u32[]{:S(2)}) collective-permute-start(bf16[2,4,2,8,1024]{4,3,2,1,0:T(8,128)(2,1)} %get-tuple-element.27), channel_id=1, source_target_pairs={{0,4},{2,6},{4,0},{6,2},{1,5},{3,7},{5,1},{7,3},{8,12},{10,14},{12... | collective-permute-start | bytes 786440 | tf_op jit(solution)/shard_map/ppermute | solution.py:388
  35.0 76.1 %collective-permute-start.2 = (bf16[2,4,2,8,1024]{4,3,2,1,0:T(8,128)(2,1)}, bf16[2,4,2,8,1024]{4,3,2,1,0:T(8,128)(2,1)}, u32[]{:S(2)}, u32[]{:S(2)}) collective-permute-start(bf16[2,4,2,8,1024]{4,3,2,1,0:T(8,128)(2,1)} %get-tuple-element.28), channel_id=1, source_target_pairs={{0,6},{2,0},{4,2},{6,4},{1,7},{3,1},{5,3},{7,5},{8,14},{10,8},{12,... | collective-permute-start | bytes 786440 | tf_op jit(solution)/shard_map/ppermute | solution.py:388
  84.2 26.9 %copy-start.1 = (bf16[2,4,2,8,1024]{4,3,2,1,0:T(8,128)(2,1)}, bf16[2,4,2,8,1024]{4,3,2,1,0:T(8,128)(2,1)S(1)}, u32[]{:S(2)}) copy-start(bf16[2,4,2,8,1024]{4,3,2,1,0:T(8,128)(2,1)S(1)} %collective-permute-done) | copy-start | bytes 786436
  113.6 6.3 %collective-permute-start.3 = (bf16[4,2,8,1024]{3,2,1,0:T(8,128)(2,1)}, bf16[4,2,8,1024]{3,2,1,0:T(8,128)(2,1)S(1)}, u32[]{:S(2)}, u32[]{:S(2)}) collective-permute-start(bf16[4,2,8,1024]{3,2,1,0:T(8,128)(2,1)} %get-tuple-element.30), channel_id=1, source_target_pairs={{0,8},{8,16},{16,24},{24,1},{1,9},{9,17},{17,25},{25,0},{2,10},{10... | collective-permute-start | bytes 393224 | tf_op jit(solution)/shard_map/ppermute | solution.py:396
  113.6 7.6 %collective-permute-start.4 = (bf16[4,2,8,1024]{3,2,1,0:T(8,128)(2,1)}, bf16[4,2,8,1024]{3,2,1,0:T(8,128)(2,1)S(1)}, u32[]{:S(2)}, u32[]{:S(2)}) collective-permute-start(bf16[4,2,8,1024]{3,2,1,0:T(8,128)(2,1)} %get-tuple-element.31), channel_id=1, source_target_pairs={{0,16},{8,24},{16,1},{24,9},{1,17},{9,25},{17,0},{25,8},{2,18},{10... | collective-permute-start | bytes 393224 | tf_op jit(solution)/shard_map/ppermute | solution.py:396
  114.6 8.4 %collective-permute-start.5 = (bf16[4,2,8,1024]{3,2,1,0:T(8,128)(2,1)}, bf16[4,2,8,1024]{3,2,1,0:T(8,128)(2,1)S(1)}, u32[]{:S(2)}, u32[]{:S(2)}) collective-permute-start(bf16[4,2,8,1024]{3,2,1,0:T(8,128)(2,1)} %get-tuple-element.32), channel_id=1, source_target_pairs={{0,24},{8,1},{16,9},{24,17},{1,25},{9,0},{17,8},{25,16},{2,26},{10... | collective-permute-start | bytes 393224 | tf_op jit(solution)/shard_map/ppermute | solution.py:396
  116.9 6.1 %collective-permute-start.6 = (bf16[4,2,8,1024]{3,2,1,0:T(8,128)(2,1)}, bf16[4,2,8,1024]{3,2,1,0:T(8,128)(2,1)}, u32[]{:S(2)}, u32[]{:S(2)}) collective-permute-start(bf16[4,2,8,1024]{3,2,1,0:T(8,128)(2,1)} %get-tuple-element.33), channel_id=1, source_target_pairs={{0,1},{8,9},{16,17},{24,25},{1,0},{9,8},{17,16},{25,24},{2,3},{10,... | collective-permute-start | bytes 393224 | tf_op jit(solution)/shard_map/ppermute | solution.py:396
  117.4 8.3 %collective-permute-start.7 = (bf16[4,2,8,1024]{3,2,1,0:T(8,128)(2,1)}, bf16[4,2,8,1024]{3,2,1,0:T(8,128)(2,1)}, u32[]{:S(2)}, u32[]{:S(2)}) collective-permute-start(bf16[4,2,8,1024]{3,2,1,0:T(8,128)(2,1)} %get-tuple-element.34), channel_id=1, source_target_pairs={{0,9},{8,17},{16,25},{24,0},{1,8},{9,16},{17,24},{25,1},{2,11},{10... | collective-permute-start | bytes 393224 | tf_op jit(solution)/shard_map/ppermute | solution.py:396
  119.9 6.9 %collective-permute-start.8 = (bf16[4,2,8,1024]{3,2,1,0:T(8,128)(2,1)}, bf16[4,2,8,1024]{3,2,1,0:T(8,128)(2,1)}, u32[]{:S(2)}, u32[]{:S(2)}) collective-permute-start(bf16[4,2,8,1024]{3,2,1,0:T(8,128)(2,1)} %get-tuple-element.35), channel_id=1, source_target_pairs={{0,17},{8,25},{16,0},{24,8},{1,16},{9,24},{17,1},{25,9},{2,19},{10... | collective-permute-start | bytes 393224 | tf_op jit(solution)/shard_map/ppermute | solution.py:396
  121.2 6.9 %collective-permute-start.9 = (bf16[4,2,8,1024]{3,2,1,0:T(8,128)(2,1)}, bf16[4,2,8,1024]{3,2,1,0:T(8,128)(2,1)}, u32[]{:S(2)}, u32[]{:S(2)}) collective-permute-start(bf16[4,2,8,1024]{3,2,1,0:T(8,128)(2,1)} %get-tuple-element.36), channel_id=1, source_target_pairs={{0,25},{8,0},{16,8},{24,16},{1,24},{9,1},{17,9},{25,17},{2,27},{10... | collective-permute-start | bytes 393224 | tf_op jit(solution)/shard_map/ppermute | solution.py:396
  132.2 47.8 %all-to-all-start = ((bf16[8,8,32,128]{3,2,1,0:T(8,128)(2,1)}), bf16[8,8,32,128]{3,2,1,0:T(8,128)(2,1)}, u32[]{:S(2)}, u32[]{:S(2)}) async-start(bf16[8,8,32,128]{3,2,1,0:T(8,128)(2,1)} %shard_map.102), calls=%async_computation | async-start | bytes 1048576 | tf_op jit(solution)/shard_map/all_to_all | solution.py:403
  147.6 11.7 %collective-permute-start.10 = (bf16[24,32,128]{2,1,0:T(8,128)(2,1)}, bf16[24,32,128]{2,1,0:T(8,128)(2,1)S(1)}, u32[]{:S(2)}, u32[]{:S(2)}) collective-permute-start(bf16[24,32,128]{2,1,0:T(8,128)(2,1)} %get-tuple-element.38), channel_id=1, source_target_pairs={{0,2},{2,4},{4,6},{6,1},{1,3},{3,5},{5,7},{7,0},{8,10},{10,12},{12... | collective-permute-start | bytes 589832 | tf_op jit(solution)/shard_map/ppermute | solution.py:408
  149.7 28.1 %collective-permute-start.11 = (bf16[24,32,128]{2,1,0:T(8,128)(2,1)}, bf16[24,32,128]{2,1,0:T(8,128)(2,1)S(1)}, u32[]{:S(2)}, u32[]{:S(2)}) collective-permute-start(bf16[24,32,128]{2,1,0:T(8,128)(2,1)} %get-tuple-element.39), channel_id=1, source_target_pairs={{0,4},{2,6},{4,1},{6,3},{1,5},{3,7},{5,0},{7,2},{8,12},{10,14},{12... | collective-permute-start | bytes 589832 | tf_op jit(solution)/shard_map/ppermute | solution.py:408
  152.0 28.0 %collective-permute-start.12 = (bf16[24,32,128]{2,1,0:T(8,128)(2,1)}, bf16[24,32,128]{2,1,0:T(8,128)(2,1)S(1)}, u32[]{:S(2)}, u32[]{:S(2)}) collective-permute-start(bf16[24,32,128]{2,1,0:T(8,128)(2,1)} %get-tuple-element.40), channel_id=1, source_target_pairs={{0,6},{2,1},{4,3},{6,5},{1,7},{3,0},{5,2},{7,4},{8,14},{10,9},{12,... | collective-permute-start | bytes 589832 | tf_op jit(solution)/shard_map/ppermute | solution.py:408
  154.4 25.6 %collective-permute-start.13 = (bf16[24,32,128]{2,1,0:T(8,128)(2,1)}, bf16[24,32,128]{2,1,0:T(8,128)(2,1)S(1)}, u32[]{:S(2)}, u32[]{:S(2)}) collective-permute-start(bf16[24,32,128]{2,1,0:T(8,128)(2,1)} %get-tuple-element.41), channel_id=1, source_target_pairs={{0,1},{2,3},{4,5},{6,7},{1,0},{3,2},{5,4},{7,6},{8,9},{10,11},{12,... | collective-permute-start | bytes 589832 | tf_op jit(solution)/shard_map/ppermute | solution.py:408
  154.9 25.1 %collective-permute-start.14 = (bf16[24,32,128]{2,1,0:T(8,128)(2,1)}, bf16[24,32,128]{2,1,0:T(8,128)(2,1)S(1)}, u32[]{:S(2)}, u32[]{:S(2)}) collective-permute-start(bf16[24,32,128]{2,1,0:T(8,128)(2,1)} %get-tuple-element.42), channel_id=1, source_target_pairs={{0,3},{2,5},{4,7},{6,0},{1,2},{3,4},{5,6},{7,1},{8,11},{10,13},{12... | collective-permute-start | bytes 589832 | tf_op jit(solution)/shard_map/ppermute | solution.py:408
  159.3 29.8 %copy-start.2 = (bf16[24,32,128]{2,1,0:T(8,128)(2,1)}, bf16[24,32,128]{2,1,0:T(8,128)(2,1)S(1)}, u32[]{:S(2)}) copy-start(bf16[24,32,128]{2,1,0:T(8,128)(2,1)S(1)} %collective-permute-done.10.refs_1_) | copy-start | bytes 589828
  159.3 26.0 %collective-permute-start.15 = (bf16[24,32,128]{2,1,0:T(8,128)(2,1)}, bf16[24,32,128]{2,1,0:T(8,128)(2,1)S(1)}, u32[]{:S(2)}, u32[]{:S(2)}) collective-permute-start(bf16[24,32,128]{2,1,0:T(8,128)(2,1)} %get-tuple-element.43), channel_id=1, source_target_pairs={{0,5},{2,7},{4,0},{6,2},{1,4},{3,6},{5,1},{7,3},{8,13},{10,15},{12... | collective-permute-start | bytes 589832 | tf_op jit(solution)/shard_map/ppermute | solution.py:408
  177.7 11.4 %copy-start.3 = (bf16[24,32,128]{2,1,0:T(8,128)(2,1)}, bf16[24,32,128]{2,1,0:T(8,128)(2,1)S(1)}, u32[]{:S(2)}) copy-start(bf16[24,32,128]{2,1,0:T(8,128)(2,1)S(1)} %collective-permute-done.11.refs_2_) | copy-start | bytes 589828
  177.7 11.4 %collective-permute-start.16 = (bf16[24,32,128]{2,1,0:T(8,128)(2,1)}, bf16[24,32,128]{2,1,0:T(8,128)(2,1)S(1)}, u32[]{:S(2)}, u32[]{:S(2)}) collective-permute-start(bf16[24,32,128]{2,1,0:T(8,128)(2,1)} %get-tuple-element.44), channel_id=1, source_target_pairs={{0,7},{2,0},{4,2},{6,4},{1,6},{3,1},{5,3},{7,5},{8,15},{10,8},{12,... | collective-permute-start | bytes 589832 | tf_op jit(solution)/shard_map/ppermute | solution.py:408
  180.0 9.2 %copy-start.4 = (bf16[24,32,128]{2,1,0:T(8,128)(2,1)}, bf16[24,32,128]{2,1,0:T(8,128)(2,1)S(1)}, u32[]{:S(2)}) copy-start(bf16[24,32,128]{2,1,0:T(8,128)(2,1)S(1)} %collective-permute-done.12.refs_3_) | copy-start | bytes 589828
  180.0 9.2 %copy-start.5 = (bf16[24,32,128]{2,1,0:T(8,128)(2,1)}, bf16[24,32,128]{2,1,0:T(8,128)(2,1)S(1)}, u32[]{:S(2)}) copy-start(bf16[24,32,128]{2,1,0:T(8,128)(2,1)S(1)} %collective-permute-done.13.refs_4_) | copy-start | bytes 589828
  (7 other events, 41.7 us)

commit v2 on v1

--- a/solution.py
+++ b/solution.py
@@ -15,7 +15,6 @@
 ROWS_ALIKE = (((1,), (1,)), ((), ()))
 WHOLE = pl.BlockSpec(memory_space=pltpu.VMEM)
 ANYWHERE = pl.BlockSpec(memory_space=pl.ANY)
-SCALARS = pl.BlockSpec(memory_space=pltpu.SMEM)
 
 ROOT = math.sqrt(0.5)
 
@@ -44,6 +43,11 @@
 FIVES = (8, {3: -1, 5: 1}, fives)
 CHUNKS = ((FOURS,), (TWOS, ONES, FIVES))
 PAD = 8
+
+
+def position():
+    row, col, group = (lax.axis_index(name) for name in ("row", "col", "freq"))
+    return col * lax.axis_size("row") + row, row, col * lax.axis_size("freq") + group
 
 
 def split(value):
@@ -71,7 +75,8 @@
     return jnp.asarray(coarse, jnp.float32), jnp.asarray(fine, jnp.float32)
 
 
-def dft_kernel(kinds, rows_apart, me, source, taps, *refs):
+def dft_kernel(kinds, rows_apart, source, taps, *refs):
+    me = position()
     tables, outs, scratch = refs[: 2 * len(kinds)], refs[2 * len(kinds) :][: rows_apart or 1], refs[2 * len(kinds) :]
     out, volts, sem, fold = scratch[len(outs) : len(outs) + 4]
     scratch = scratch[len(outs) + 4 :]
@@ -79,7 +84,7 @@
     eighth = length // 8
     tap_count = taps.shape[0]
     spec_count = frames - tap_count + 1
-    step, lanes, stages = 16, 128, sem.shape[0]
+    step, lanes, stages = 32, 128, sem.shape[0]
     rows, tiles = step * inputs, eighth // lanes
     bounds = [spec_count * x // stages + (tap_count - 1 if x else 0) for x in range(stages + 1)]
     copies = []
@@ -162,11 +167,11 @@
         copy.wait()
 
 
-def dft(volts, taps, me, kinds, groups, owners, rows_apart):
+def dft(volts, taps, kinds, groups, owners, rows_apart):
     frames, inputs, length = volts.shape
     width = inputs * (frames - taps.shape[0] + 1)
     channels = length // 2
-    operands, scratch, count, pieces, flops = [me, volts, taps], [], 0, 0, 0
+    operands, scratch, count, pieces, flops = [volts, taps], [], 0, 0, 0
     for kind in kinds:
         operands += angle_tables(length, channels, kind)
         folded, rows = length // 4, 2 * len(places(kind, channels))
@@ -178,7 +183,7 @@
     out_shape = jax.ShapeDtypeStruct((owners // (rows_apart or 1),) + shape[1:] if rows_apart else shape, jnp.bfloat16)
     return pl.pallas_call(
         functools.partial(dft_kernel, kinds, rows_apart),
-        in_specs=[SCALARS, ANYWHERE] + [WHOLE] * (len(operands) - 2),
+        in_specs=[ANYWHERE] + [WHOLE] * (len(operands) - 1),
         out_specs=[ANYWHERE] * (rows_apart or 1),
         out_shape=[out_shape] * (rows_apart or 1),
         scratch_shapes=[
@@ -194,7 +199,8 @@
     )(*operands)
 
 
-def turn_kernel(me, *refs):
+def turn_kernel(*refs):
+    me = position()
     sem = refs[-1]
     plane, rows = sem.shape
     blocks, outs = refs[:rows], refs[rows:-1]
@@ -210,19 +216,20 @@
         copy.wait()
 
 
-def turn(blocks, me):
+def turn(blocks):
     plane, rows = blocks[0].shape[0], len(blocks)
     shape = jax.ShapeDtypeStruct((rows,) + blocks[0].shape[1:], jnp.bfloat16)
     return pl.pallas_call(
         turn_kernel,
-        in_specs=[SCALARS] + [WHOLE] * rows,
+        in_specs=[WHOLE] * rows,
         out_specs=[ANYWHERE] * plane,
         out_shape=[shape] * plane,
         scratch_shapes=[pltpu.SemaphoreType.DMA((plane, rows))],
-    )(me, *blocks)
-
-
-def correlate_kernel(sizes, count, me, *refs):
+    )(*blocks)
+
+
+def correlate_kernel(sizes, count, *refs):
+    me = position()
     cols, rows, groups, inputs = sizes
     sources = cols * rows * groups
     out, scratch, sem = refs[-2], refs[-3], refs[-1]
@@ -278,7 +285,7 @@
         copy.wait()
 
 
-def correlate(got, me, sizes, apart):
+def correlate(got, sizes, apart):
     cols, rows, groups, inputs = sizes
     sources = cols * rows * groups
     count, width = got[0].shape[-2:]
@@ -286,7 +293,7 @@
     shape = (cols * rows, count, cols * block, 2 * rows * block)
     return pl.pallas_call(
         functools.partial(correlate_kernel, sizes, count),
-        in_specs=[SCALARS] + [WHOLE] * len(got),
+        in_specs=[WHOLE] * len(got),
         out_specs=[pl.BlockSpec(memory_space=pl.ANY)] * (shape[0] if apart else 1),
         out_shape=[jax.ShapeDtypeStruct(shape[1:] if apart else shape, jnp.bfloat16)] * (shape[0] if apart else 1),
         scratch_shapes=[
@@ -299,10 +306,11 @@
             bytes_accessed=4 * sources * count * width + 2 * math.prod(shape),
             transcendentals=0,
         ),
-    )(me, *got)
-
-
-def finish_kernel(sizes, me, first, *refs):
+    )(*got)
+
+
+def finish_kernel(sizes, first, *refs):
+    me = position()
     pieces, (same, out, scratch, held, sem) = refs[:-5], refs[-5:]
     cols, rows, groups, inputs = sizes
     owners, _, width, lanes = first.shape
@@ -349,20 +357,20 @@
         copy.wait()
 
 
-def finish(first, pieces, me, sizes):
+def finish(first, pieces, sizes):
     cols, rows, groups, inputs = sizes
     owners, _, width, lanes = first.shape
     total = first.shape[1] + pieces[0].shape[0]
     channels = owners * total
     if channels % 128 or 128 % (rows * groups):
         order = np.argsort(sum((places(kind, total) for kinds in CHUNKS for kind in kinds), []))
-        second = jnp.stack(pieces)[(me[0] - jnp.arange(owners)) % owners]
+        second = jnp.stack(pieces)[(position()[0] - jnp.arange(owners)) % owners]
         value = jnp.concatenate([first, second], axis=1)[:, order]
         value = value.reshape(channels, inputs, cols, groups, 2, inputs, rows, groups)
         return value.transpose(4, 6, 7, 5, 2, 3, 1, 0).reshape(lanes * width, channels).astype(jnp.float32)
     return pl.pallas_call(
         functools.partial(finish_kernel, sizes),
-        in_specs=[pl.BlockSpec(memory_space=pltpu.SMEM)] + [WHOLE] * (owners + 2),
+        in_specs=[WHOLE] * (owners + 2),
         out_specs=pl.BlockSpec(memory_space=pl.ANY),
         out_shape=jax.ShapeDtypeStruct((2 * rows * groups, inputs * width, channels), jnp.float32),
         scratch_shapes=[
@@ -370,7 +378,7 @@
             pltpu.VMEM((channels // 128, 2 * rows * groups, inputs * width + PAD, 128), jnp.float32),
             pltpu.SemaphoreType.DMA((channels // 128,)),
         ],
-    )(me, first, *pieces, jnp.eye(128, dtype=jnp.bfloat16))
+    )(first, *pieces, jnp.eye(128, dtype=jnp.bfloat16))
 
 
 def shards(voltages, tap_table):
@@ -380,33 +388,31 @@
     volts = voltages.transpose(1, 0, 2)
     owners = rows * cols
     plane = cols * groups
-    row, col, group = (lax.axis_index(name) for name in ("row", "col", "freq"))
-    me = jnp.stack([col * rows + row, row, col * groups + group]).astype(jnp.int32)
-
-    blocks = list(dft(volts, tap_table, me, CHUNKS[0], groups, owners, rows))
+
+    blocks = list(dft(volts, tap_table, CHUNKS[0], groups, owners, rows))
     for k in range(1, rows):
         blocks[k] = lax.ppermute(blocks[k], "row", [(x, (x + k) % rows) for x in range(rows)])
-    sent = dft(volts, tap_table, me, CHUNKS[1], groups, owners, 0)[0]
+    sent = dft(volts, tap_table, CHUNKS[1], groups, owners, 0)[0]
     sent = sent.reshape((-1,) + sent.shape[2:])
     second = lax.all_to_all(sent, EVERYONE, split_axis=0, concat_axis=0, tiled=True)
-    blocks = list(turn([x.reshape((plane,) + x.shape[2:]) for x in blocks], me))
+    blocks = list(turn([x.reshape((plane,) + x.shape[2:]) for x in blocks]))
     meshed = lambda place: place % groups * cols + place // groups
     for q in range(1, plane):
         pairs = [(meshed(x), meshed((x + q) % plane)) for x in range(plane)]
         blocks[q] = lax.ppermute(blocks[q], ("freq", "col"), pairs)
     if blocks[0].shape[2] % 8:
-        stacked = jnp.stack(blocks)[(me[2] - jnp.arange(plane)) % plane]
+        stacked = jnp.stack(blocks)[(position()[2] - jnp.arange(plane)) % plane]
         stacked = stacked.reshape((cols, groups) + stacked.shape[1:]).swapaxes(1, 2)
         blocks = [stacked.reshape((-1,) + stacked.shape[3:])]
 
-    first = correlate(blocks, me, sizes, False)[0]
+    first = correlate(blocks, sizes, False)[0]
     first = lax.all_to_all(first, OWNERS, split_axis=0, concat_axis=0, tiled=True)
-    pieces = list(correlate([second], me, sizes, True))
+    pieces = list(correlate([second], sizes, True))
     meshed = lambda owner: owner % rows * cols + owner // rows
     for k in range(1, owners):
         pairs = [(meshed(x), meshed((x + k) % owners)) for x in range(owners)]
         pieces[k] = lax.ppermute(pieces[k], OWNERS[::-1], pairs)
-    result = finish(first, pieces, me, sizes)
+    result = finish(first, pieces, sizes)
     block = groups * inputs
     return result.reshape(2, rows, block, cols * block, -1).transpose(4, 0, 1, 2, 3)
 

time: 195 us -> 194 us (level)
  no operation moved by 1% of the time
where the time goes in v2:
time: 194 us
  waiting for transfers between devices  103 us (53%)
  starting transfers between devices  48.7 us (25%)
  Pallas kernels  41 us (21%)
    ppermute x3, waiting for transfers between devices, shards(): lax.ppermute(blocks[k], 'row', [(x, (x + k) % rows) for x in range(rows)])  74.9 us
    pallas_call x2, Pallas kernels, dft(): pl.pallas_call(functools.partial(dft_kernel, kinds, rows_apart), in_specs...  22.3 us
    ppermute x7, starting transfers between devices, shards(): pieces[k] = lax.ppermute(pieces[k], OWNERS[::-1], pairs)  21.2 us
    ppermute x7, waiting for transfers between devices, shards(): pieces[k] = lax.ppermute(pieces[k], OWNERS[::-1], pairs)  19.7 us
    pallas_call x2, Pallas kernels, correlate(): pl.pallas_call(functools.partial(correlate_kernel, sizes, count), in_spec...  11.3 us
    all_to_all x1, starting transfers between devices, shards(): lax.all_to_all(first, OWNERS, split_axis=0, concat_axis=0, tiled=True)  7.99 us
    ppermute x7, waiting for transfers between devices, shards(): blocks[q] = lax.ppermute(blocks[q], ('freq', 'col'), pairs)  7.9 us
    all_to_all x1, starting transfers between devices, shards(): lax.all_to_all(sent, EVERYONE, split_axis=0, concat_axis=0, tiled=True)  7.33 us
  transfers between devices with their start and end apart: 19, of which 11 were waited for; matrix products, arithmetic and copies ran while one was open for 0% of the time, Pallas kernels for 12%

profile of v2, /device:TPU:0, one launch (start us, length us, event | category | flops | bytes accessed | tf_op | source)
XLA Modules:
  0.0 193.9 jit_solution(7134075318202617848)
XLA Ops:
  0.0 13.5 %shard_map.103 = bf16[8,4,2,24,1024]{4,3,2,1,0:T(8,128)(2,1)} custom-call(bf16[259,4,2048]{2,1,0:T(4,128)(2,1)} %bitcast.12, s32[4,2048]{1,0:T(4,128)} %taps.3, f32[2,32,512]{2,1,0:T(8,128)} %constant.12.clone.refs_0_, f32[3,8,512]{2,1,0:T(8,128)} %constant.14.clone.refs_1_, f32[2,32,256]{2,1,0:T(8,128)} %constant.15.clone.refs_2_.refs_4_, ...), custom_call_target="tpu_custom_call" | custom-call | flops 4831838208 | bytes 7389184 | tf_op jit(solution)/shard_map/pallas_call | solution.py:184
  13.5 7.3 %all-to-all-start.1 = ((bf16[32,2,24,1024]{3,2,1,0:T(8,128)(2,1)}), bf16[32,2,24,1024]{3,2,1,0:T(8,128)(2,1)S(1)}, u32[]{:S(2)}, u32[]{:S(2)}) async-start(bf16[32,2,24,1024]{3,2,1,0:T(8,128)(2,1)} %bitcast.9), calls=%async_computation.1 | async-start | bytes 6291456 | tf_op jit(solution)/shard_map/all_to_all | solution.py:397
  20.8 8.8 %shard_map.100 = (bf16[2,4,2,8,1024]{4,3,2,1,0:T(8,128)(2,1)}, bf16[2,4,2,8,1024]{4,3,2,1,0:T(8,128)(2,1)}, bf16[2,4,2,8,1024]{4,3,2,1,0:T(8,128)(2,1)}, bf16[2,4,2,8,1024]{4,3,2,1,0:T(8,128)(2,1)}) custom-call(bf16[259,4,2048]{2,1,0:T(4,128)(2,1)} %bitcast.13, s32[4,2048]{1,0:T(4,128)} %taps.3, f32[2,32,512]{2,1,0:T(8,128)} %constant.12.clone.refs_0_, ...), custom_call_target="tpu_custom_call" | custom-call | flops 1610612736 | bytes 5292032 | tf_op jit(solution)/shard_map/pallas_call | solution.py:184
  29.6 1.8 collective-permute-start
  31.5 2.4 %collective-permute-start.1 = (bf16[2,4,2,8,1024]{4,3,2,1,0:T(8,128)(2,1)}, bf16[2,4,2,8,1024]{4,3,2,1,0:T(8,128)(2,1)}, u32[]{:S(2)}, u32[]{:S(2)}) collective-permute-start(bf16[2,4,2,8,1024]{4,3,2,1,0:T(8,128)(2,1)} %get-tuple-element.27), channel_id=1, source_target_pairs={{0,4},{2,6},{4,0},{6,2},{1,5},{3,7},{5,1},{7,3},{8,12},{10,14},{12... | collective-permute-start | bytes 786440 | tf_op jit(solution)/shard_map/ppermute | solution.py:394
  35.3 48.1 %collective-permute-done = bf16[2,4,2,8,1024]{4,3,2,1,0:T(8,128)(2,1)S(1)} collective-permute-done((bf16[2,4,2,8,1024]{4,3,2,1,0:T(8,128)(2,1)}, bf16[2,4,2,8,1024]{4,3,2,1,0:T(8,128)(2,1)S(1)}, u32[]{:S(2)}, u32[]{:S(2)}) %collective-permute-start) | collective-permute-done | bytes 262176 | tf_op jit(solution)/shard_map/ppermute | solution.py:394
  83.4 26.9 %collective-permute-done.1 = bf16[2,4,2,8,1024]{4,3,2,1,0:T(8,128)(2,1)} collective-permute-done((bf16[2,4,2,8,1024]{4,3,2,1,0:T(8,128)(2,1)}, bf16[2,4,2,8,1024]{4,3,2,1,0:T(8,128)(2,1)}, u32[]{:S(2)}, u32[]{:S(2)}) %collective-permute-start.1) | collective-permute-done | bytes 262176 | tf_op jit(solution)/shard_map/ppermute | solution.py:394
  110.2 2.4 %shard_map.101 = (bf16[4,2,8,1024]{3,2,1,0:T(8,128)(2,1)}, bf16[4,2,8,1024]{3,2,1,0:T(8,128)(2,1)}, bf16[4,2,8,1024]{3,2,1,0:T(8,128)(2,1)}, bf16[4,2,8,1024]{3,...) custom-call(bf16[8,2,8,1024]{3,2,1,0:T(8,128)(2,1)} %bitcast.10, ...), custom_call_target="tpu_custom_call" | custom-call | tf_op jit(solution)/shard_map/pallas_call | solution.py:222
  113.7 2.3 %collective-permute-start.5 = (bf16[4,2,8,1024]{3,2,1,0:T(8,128)(2,1)}, bf16[4,2,8,1024]{3,2,1,0:T(8,128)(2,1)S(1)}, u32[]{:S(2)}, u32[]{:S(2)}) collective-permute-start(bf16[4,2,8,1024]{3,2,1,0:T(8,128)(2,1)} %get-tuple-element.32), channel_id=1, source_target_pairs={{0,24},{8,1},{16,9},{24,17},{1,25},{9,0},{17,8},{25,16},{2,26},{10... | collective-permute-start | bytes 393224 | tf_op jit(solution)/shard_map/ppermute | solution.py:402
  116.6 2.4 %collective-permute-done.3.refs_1_ = bf16[4,2,8,1024]{3,2,1,0:T(8,128)(2,1)S(1)} collective-permute-done((bf16[4,2,8,1024]{3,2,1,0:T(8,128)(2,1)}, bf16[4,2,8,1024]{3,2,1,0:T(8,128)(2,1)S(1)}, u32[]{:S(2)}, u32[]{:S(2)}) %collective-permute-start.3) | collective-permute-done | bytes 131104 | tf_op jit(solution)/shard_map/ppermute | solution.py:402
  120.3 1.8 collective-permute-start.9
  122.1 2.7 %collective-permute-done.7.refs_5_ = bf16[4,2,8,1024]{3,2,1,0:T(8,128)(2,1)} collective-permute-done((bf16[4,2,8,1024]{3,2,1,0:T(8,128)(2,1)}, bf16[4,2,8,1024]{3,2,1,0:T(8,128)(2,1)}, u32[]{:S(2)}, u32[]{:S(2)}) %collective-permute-start.7) | collective-permute-done | bytes 131104 | tf_op jit(solution)/shard_map/ppermute | solution.py:402
  127.2 3.7 %shard_map.102 = bf16[8,8,32,128]{3,2,1,0:T(8,128)(2,1)} custom-call(bf16[4,2,8,1024]{3,2,1,0:T(8,128)(2,1)} %get-tuple-element.29.refs_0_, bf16[4,2,8,1024]{3,2,1,0:T(8,128)(2,1)} %copy-done.9, bf16[4,2,8,1024]{3,2,1,0:T(8,128)(2,1)} %copy-done.10, bf16[4,2,8,1024]{3,2,1,0:T(8,128)(2,1)} %copy-done.11, ...), custom_call_target="tpu_custom_call" | custom-call | flops 268435456 | bytes 1572864 | tf_op jit(solution)/shard_map/pallas_call | solution.py:294
  130.9 8.0 %all-to-all-start = ((bf16[8,8,32,128]{3,2,1,0:T(8,128)(2,1)}), bf16[8,8,32,128]{3,2,1,0:T(8,128)(2,1)}, u32[]{:S(2)}, u32[]{:S(2)}) async-start(bf16[8,8,32,128]{3,2,1,0:T(8,128)(2,1)} %shard_map.102), calls=%async_computation | async-start | bytes 1048576 | tf_op jit(solution)/shard_map/all_to_all | solution.py:409
  138.9 7.6 %shard_map.104 = (bf16[24,32,128]{2,1,0:T(8,128)(2,1)}, bf16[24,32,128]{2,1,0:T(8,128)(2,1)}, bf16[24,32,128]{2,1,0:T(8,128)(2,1)}, bf16[24,32,128]{2,1,0:T(8,12...) custom-call(bf16[32,2,24,1024]{3,2,1,0:T(8,128)(2,1)} %copy-done), custom_call_target="tpu_custom_call" | custom-call | flops 805306368 | bytes 4718592 | tf_op jit(solution)/shard_map/pallas_call | solution.py:294
  146.5 2.1 %collective-permute-start.10 = (bf16[24,32,128]{2,1,0:T(8,128)(2,1)}, bf16[24,32,128]{2,1,0:T(8,128)(2,1)S(1)}, u32[]{:S(2)}, u32[]{:S(2)}) collective-permute-start(bf16[24,32,128]{2,1,0:T(8,128)(2,1)} %get-tuple-element.38), channel_id=1, source_target_pairs={{0,2},{2,4},{4,6},{6,1},{1,3},{3,5},{5,7},{7,0},{8,10},{10,12},{12... | collective-permute-start | bytes 589832 | tf_op jit(solution)/shard_map/ppermute | solution.py:414
  148.6 2.4 %collective-permute-start.11 = (bf16[24,32,128]{2,1,0:T(8,128)(2,1)}, bf16[24,32,128]{2,1,0:T(8,128)(2,1)S(1)}, u32[]{:S(2)}, u32[]{:S(2)}) collective-permute-start(bf16[24,32,128]{2,1,0:T(8,128)(2,1)} %get-tuple-element.39), channel_id=1, source_target_pairs={{0,4},{2,6},{4,1},{6,3},{1,5},{3,7},{5,0},{7,2},{8,12},{10,14},{12... | collective-permute-start | bytes 589832 | tf_op jit(solution)/shard_map/ppermute | solution.py:414
  150.9 2.4 %collective-permute-start.12 = (bf16[24,32,128]{2,1,0:T(8,128)(2,1)}, bf16[24,32,128]{2,1,0:T(8,128)(2,1)S(1)}, u32[]{:S(2)}, u32[]{:S(2)}) collective-permute-start(bf16[24,32,128]{2,1,0:T(8,128)(2,1)} %get-tuple-element.40), channel_id=1, source_target_pairs={{0,6},{2,1},{4,3},{6,5},{1,7},{3,0},{5,2},{7,4},{8,14},{10,9},{12,... | collective-permute-start | bytes 589832 | tf_op jit(solution)/shard_map/ppermute | solution.py:414
  155.3 2.9 %collective-permute-done.10.refs_1_ = bf16[24,32,128]{2,1,0:T(8,128)(2,1)S(1)} collective-permute-done((bf16[24,32,128]{2,1,0:T(8,128)(2,1)}, bf16[24,32,128]{2,1,0:T(8,128)(2,1)S(1)}, u32[]{:S(2)}, u32[]{:S(2)}) %collective-permute-start.10) | collective-permute-done | bytes 196640 | tf_op jit(solution)/shard_map/ppermute | solution.py:414
  158.2 10.7 %collective-permute-start.15 = (bf16[24,32,128]{2,1,0:T(8,128)(2,1)}, bf16[24,32,128]{2,1,0:T(8,128)(2,1)S(1)}, u32[]{:S(2)}, u32[]{:S(2)}) collective-permute-start(bf16[24,32,128]{2,1,0:T(8,128)(2,1)} %get-tuple-element.43), channel_id=1, source_target_pairs={{0,5},{2,7},{4,0},{6,2},{1,4},{3,6},{5,1},{7,3},{8,13},{10,15},{12... | collective-permute-start | bytes 589832 | tf_op jit(solution)/shard_map/ppermute | solution.py:414
  169.0 7.7 %collective-permute-done.11.refs_2_ = bf16[24,32,128]{2,1,0:T(8,128)(2,1)S(1)} collective-permute-done((bf16[24,32,128]{2,1,0:T(8,128)(2,1)}, bf16[24,32,128]{2,1,0:T(8,128)(2,1)S(1)}, u32[]{:S(2)}, u32[]{:S(2)}) %collective-permute-start.11) | collective-permute-done | bytes 196640 | tf_op jit(solution)/shard_map/ppermute | solution.py:414
  179.0 5.3 %collective-permute-done.15.refs_6_ = bf16[24,32,128]{2,1,0:T(8,128)(2,1)S(1)} collective-permute-done((bf16[24,32,128]{2,1,0:T(8,128)(2,1)}, bf16[24,32,128]{2,1,0:T(8,128)(2,1)S(1)}, u32[]{:S(2)}, u32[]{:S(2)}) %collective-permute-start.15) | collective-permute-done | bytes 196640 | tf_op jit(solution)/shard_map/ppermute | solution.py:414
  184.3 3.8 %collective-permute-done.16.refs_7_ = bf16[24,32,128]{2,1,0:T(8,128)(2,1)S(1)} collective-permute-done((bf16[24,32,128]{2,1,0:T(8,128)(2,1)}, bf16[24,32,128]{2,1,0:T(8,128)(2,1)S(1)}, u32[]{:S(2)}, u32[]{:S(2)}) %collective-permute-start.16) | collective-permute-done | bytes 196640 | tf_op jit(solution)/shard_map/ppermute | solution.py:414
  188.8 5.0 %shard_map.105 = f32[32,128,256]{2,1,0:T(8,128)} custom-call(bf16[8,8,32,128]{3,2,1,0:T(8,128)(2,1)} %all-to-all-done.first, bf16[24,32,128]{2,1,0:T(8,128)(2,1)} %get-tuple-element.37.refs_0_, bf16[24,32,128]{2,1,0:T(8,128)(2,1)} %copy-done.2, bf16[24,32,128]{2,1,0:T(8,128)(2,1)} %copy-done.3, bf16[24,32,128]{2,1,0:T(8,128)(2,1)} %copy-done.4, ...), custom_call_target="tpu_custom_call" | custom-call | tf_op jit(solution)/shard_map/pallas_call | solution.py:371
  (45 shorter events, 11.7 us)
Async XLA Ops:
  13.5 117.4 %all-to-all-start.1 = ((bf16[32,2,24,1024]{3,2,1,0:T(8,128)(2,1)}), bf16[32,2,24,1024]{3,2,1,0:T(8,128)(2,1)S(1)}, u32[]{:S(2)}, u32[]{:S(2)}) async-start(bf16[32,2,24,1024]{3,2,1,0:T(8,128)(2,1)} %bitcast.9), calls=%async_computation.1 | async-start | bytes 6291456 | tf_op jit(solution)/shard_map/all_to_all | solution.py:397
  29.6 53.7 %collective-permute-start = (bf16[2,4,2,8,1024]{4,3,2,1,0:T(8,128)(2,1)}, bf16[2,4,2,8,1024]{4,3,2,1,0:T(8,128)(2,1)S(1)}, u32[]{:S(2)}, u32[]{:S(2)}) collective-permute-start(bf16[2,4,2,8,1024]{4,3,2,1,0:T(8,128)(2,1)} %get-tuple-element.26), channel_id=1, source_target_pairs={{0,2},{2,4},{4,6},{6,0},{1,3},{3,5},{5,7},{7,1},{8,10},{10,12},{12... | collective-permute-start | bytes 786440 | tf_op jit(solution)/shard_map/ppermute | solution.py:394
  31.5 78.8 %collective-permute-start.1 = (bf16[2,4,2,8,1024]{4,3,2,1,0:T(8,128)(2,1)}, bf16[2,4,2,8,1024]{4,3,2,1,0:T(8,128)(2,1)}, u32[]{:S(2)}, u32[]{:S(2)}) collective-permute-start(bf16[2,4,2,8,1024]{4,3,2,1,0:T(8,128)(2,1)} %get-tuple-element.27), channel_id=1, source_target_pairs={{0,4},{2,6},{4,0},{6,2},{1,5},{3,7},{5,1},{7,3},{8,12},{10,14},{12... | collective-permute-start | bytes 786440 | tf_op jit(solution)/shard_map/ppermute | solution.py:394
  33.9 76.4 %collective-permute-start.2 = (bf16[2,4,2,8,1024]{4,3,2,1,0:T(8,128)(2,1)}, bf16[2,4,2,8,1024]{4,3,2,1,0:T(8,128)(2,1)}, u32[]{:S(2)}, u32[]{:S(2)}) collective-permute-start(bf16[2,4,2,8,1024]{4,3,2,1,0:T(8,128)(2,1)} %get-tuple-element.28), channel_id=1, source_target_pairs={{0,6},{2,0},{4,2},{6,4},{1,7},{3,1},{5,3},{7,5},{8,14},{10,8},{12,... | collective-permute-start | bytes 786440 | tf_op jit(solution)/shard_map/ppermute | solution.py:394
  83.4 26.9 %copy-start.1 = (bf16[2,4,2,8,1024]{4,3,2,1,0:T(8,128)(2,1)}, bf16[2,4,2,8,1024]{4,3,2,1,0:T(8,128)(2,1)S(1)}, u32[]{:S(2)}) copy-start(bf16[2,4,2,8,1024]{4,3,2,1,0:T(8,128)(2,1)S(1)} %collective-permute-done) | copy-start | bytes 786436
  112.7 6.3 %collective-permute-start.3 = (bf16[4,2,8,1024]{3,2,1,0:T(8,128)(2,1)}, bf16[4,2,8,1024]{3,2,1,0:T(8,128)(2,1)S(1)}, u32[]{:S(2)}, u32[]{:S(2)}) collective-permute-start(bf16[4,2,8,1024]{3,2,1,0:T(8,128)(2,1)} %get-tuple-element.30), channel_id=1, source_target_pairs={{0,8},{8,16},{16,24},{24,1},{1,9},{9,17},{17,25},{25,0},{2,10},{10... | collective-permute-start | bytes 393224 | tf_op jit(solution)/shard_map/ppermute | solution.py:402
  112.8 7.6 %collective-permute-start.4 = (bf16[4,2,8,1024]{3,2,1,0:T(8,128)(2,1)}, bf16[4,2,8,1024]{3,2,1,0:T(8,128)(2,1)S(1)}, u32[]{:S(2)}, u32[]{:S(2)}) collective-permute-start(bf16[4,2,8,1024]{3,2,1,0:T(8,128)(2,1)} %get-tuple-element.31), channel_id=1, source_target_pairs={{0,16},{8,24},{16,1},{24,9},{1,17},{9,25},{17,0},{25,8},{2,18},{10... | collective-permute-start | bytes 393224 | tf_op jit(solution)/shard_map/ppermute | solution.py:402
  113.7 8.4 %collective-permute-start.5 = (bf16[4,2,8,1024]{3,2,1,0:T(8,128)(2,1)}, bf16[4,2,8,1024]{3,2,1,0:T(8,128)(2,1)S(1)}, u32[]{:S(2)}, u32[]{:S(2)}) collective-permute-start(bf16[4,2,8,1024]{3,2,1,0:T(8,128)(2,1)} %get-tuple-element.32), channel_id=1, source_target_pairs={{0,24},{8,1},{16,9},{24,17},{1,25},{9,0},{17,8},{25,16},{2,26},{10... | collective-permute-start | bytes 393224 | tf_op jit(solution)/shard_map/ppermute | solution.py:402
  116.0 6.1 %collective-permute-start.6 = (bf16[4,2,8,1024]{3,2,1,0:T(8,128)(2,1)}, bf16[4,2,8,1024]{3,2,1,0:T(8,128)(2,1)}, u32[]{:S(2)}, u32[]{:S(2)}) collective-permute-start(bf16[4,2,8,1024]{3,2,1,0:T(8,128)(2,1)} %get-tuple-element.33), channel_id=1, source_target_pairs={{0,1},{8,9},{16,17},{24,25},{1,0},{9,8},{17,16},{25,24},{2,3},{10,... | collective-permute-start | bytes 393224 | tf_op jit(solution)/shard_map/ppermute | solution.py:402
  116.5 8.3 %collective-permute-start.7 = (bf16[4,2,8,1024]{3,2,1,0:T(8,128)(2,1)}, bf16[4,2,8,1024]{3,2,1,0:T(8,128)(2,1)}, u32[]{:S(2)}, u32[]{:S(2)}) collective-permute-start(bf16[4,2,8,1024]{3,2,1,0:T(8,128)(2,1)} %get-tuple-element.34), channel_id=1, source_target_pairs={{0,9},{8,17},{16,25},{24,0},{1,8},{9,16},{17,24},{25,1},{2,11},{10... | collective-permute-start | bytes 393224 | tf_op jit(solution)/shard_map/ppermute | solution.py:402
  119.0 6.9 %collective-permute-start.8 = (bf16[4,2,8,1024]{3,2,1,0:T(8,128)(2,1)}, bf16[4,2,8,1024]{3,2,1,0:T(8,128)(2,1)}, u32[]{:S(2)}, u32[]{:S(2)}) collective-permute-start(bf16[4,2,8,1024]{3,2,1,0:T(8,128)(2,1)} %get-tuple-element.35), channel_id=1, source_target_pairs={{0,17},{8,25},{16,0},{24,8},{1,16},{9,24},{17,1},{25,9},{2,19},{10... | collective-permute-start | bytes 393224 | tf_op jit(solution)/shard_map/ppermute | solution.py:402
  120.3 6.9 %collective-permute-start.9 = (bf16[4,2,8,1024]{3,2,1,0:T(8,128)(2,1)}, bf16[4,2,8,1024]{3,2,1,0:T(8,128)(2,1)}, u32[]{:S(2)}, u32[]{:S(2)}) collective-permute-start(bf16[4,2,8,1024]{3,2,1,0:T(8,128)(2,1)} %get-tuple-element.36), channel_id=1, source_target_pairs={{0,25},{8,0},{16,8},{24,16},{1,24},{9,1},{17,9},{25,17},{2,27},{10... | collective-permute-start | bytes 393224 | tf_op jit(solution)/shard_map/ppermute | solution.py:402
  130.9 48.0 %all-to-all-start = ((bf16[8,8,32,128]{3,2,1,0:T(8,128)(2,1)}), bf16[8,8,32,128]{3,2,1,0:T(8,128)(2,1)}, u32[]{:S(2)}, u32[]{:S(2)}) async-start(bf16[8,8,32,128]{3,2,1,0:T(8,128)(2,1)} %shard_map.102), calls=%async_computation | async-start | bytes 1048576 | tf_op jit(solution)/shard_map/all_to_all | solution.py:409
  146.5 11.7 %collective-permute-start.10 = (bf16[24,32,128]{2,1,0:T(8,128)(2,1)}, bf16[24,32,128]{2,1,0:T(8,128)(2,1)S(1)}, u32[]{:S(2)}, u32[]{:S(2)}) collective-permute-start(bf16[24,32,128]{2,1,0:T(8,128)(2,1)} %get-tuple-element.38), channel_id=1, source_target_pairs={{0,2},{2,4},{4,6},{6,1},{1,3},{3,5},{5,7},{7,0},{8,10},{10,12},{12... | collective-permute-start | bytes 589832 | tf_op jit(solution)/shard_map/ppermute | solution.py:414
  148.6 28.1 %collective-permute-start.11 = (bf16[24,32,128]{2,1,0:T(8,128)(2,1)}, bf16[24,32,128]{2,1,0:T(8,128)(2,1)S(1)}, u32[]{:S(2)}, u32[]{:S(2)}) collective-permute-start(bf16[24,32,128]{2,1,0:T(8,128)(2,1)} %get-tuple-element.39), channel_id=1, source_target_pairs={{0,4},{2,6},{4,1},{6,3},{1,5},{3,7},{5,0},{7,2},{8,12},{10,14},{12... | collective-permute-start | bytes 589832 | tf_op jit(solution)/shard_map/ppermute | solution.py:414
  150.9 28.0 %collective-permute-start.12 = (bf16[24,32,128]{2,1,0:T(8,128)(2,1)}, bf16[24,32,128]{2,1,0:T(8,128)(2,1)S(1)}, u32[]{:S(2)}, u32[]{:S(2)}) collective-permute-start(bf16[24,32,128]{2,1,0:T(8,128)(2,1)} %get-tuple-element.40), channel_id=1, source_target_pairs={{0,6},{2,1},{4,3},{6,5},{1,7},{3,0},{5,2},{7,4},{8,14},{10,9},{12,... | collective-permute-start | bytes 589832 | tf_op jit(solution)/shard_map/ppermute | solution.py:414
  153.3 25.6 %collective-permute-start.13 = (bf16[24,32,128]{2,1,0:T(8,128)(2,1)}, bf16[24,32,128]{2,1,0:T(8,128)(2,1)S(1)}, u32[]{:S(2)}, u32[]{:S(2)}) collective-permute-start(bf16[24,32,128]{2,1,0:T(8,128)(2,1)} %get-tuple-element.41), channel_id=1, source_target_pairs={{0,1},{2,3},{4,5},{6,7},{1,0},{3,2},{5,4},{7,6},{8,9},{10,11},{12,... | collective-permute-start | bytes 589832 | tf_op jit(solution)/shard_map/ppermute | solution.py:414
  153.9 25.1 %collective-permute-start.14 = (bf16[24,32,128]{2,1,0:T(8,128)(2,1)}, bf16[24,32,128]{2,1,0:T(8,128)(2,1)S(1)}, u32[]{:S(2)}, u32[]{:S(2)}) collective-permute-start(bf16[24,32,128]{2,1,0:T(8,128)(2,1)} %get-tuple-element.42), channel_id=1, source_target_pairs={{0,3},{2,5},{4,7},{6,0},{1,2},{3,4},{5,6},{7,1},{8,11},{10,13},{12... | collective-permute-start | bytes 589832 | tf_op jit(solution)/shard_map/ppermute | solution.py:414
  158.2 29.8 %copy-start.2 = (bf16[24,32,128]{2,1,0:T(8,128)(2,1)}, bf16[24,32,128]{2,1,0:T(8,128)(2,1)S(1)}, u32[]{:S(2)}) copy-start(bf16[24,32,128]{2,1,0:T(8,128)(2,1)S(1)} %collective-permute-done.10.refs_1_) | copy-start | bytes 589828
  158.2 26.0 %collective-permute-start.15 = (bf16[24,32,128]{2,1,0:T(8,128)(2,1)}, bf16[24,32,128]{2,1,0:T(8,128)(2,1)S(1)}, u32[]{:S(2)}, u32[]{:S(2)}) collective-permute-start(bf16[24,32,128]{2,1,0:T(8,128)(2,1)} %get-tuple-element.43), channel_id=1, source_target_pairs={{0,5},{2,7},{4,0},{6,2},{1,4},{3,6},{5,1},{7,3},{8,13},{10,15},{12... | collective-permute-start | bytes 589832 | tf_op jit(solution)/shard_map/ppermute | solution.py:414
  176.6 11.4 %copy-start.3 = (bf16[24,32,128]{2,1,0:T(8,128)(2,1)}, bf16[24,32,128]{2,1,0:T(8,128)(2,1)S(1)}, u32[]{:S(2)}) copy-start(bf16[24,32,128]{2,1,0:T(8,128)(2,1)S(1)} %collective-permute-done.11.refs_2_) | copy-start | bytes 589828
  176.7 11.4 %collective-permute-start.16 = (bf16[24,32,128]{2,1,0:T(8,128)(2,1)}, bf16[24,32,128]{2,1,0:T(8,128)(2,1)S(1)}, u32[]{:S(2)}, u32[]{:S(2)}) collective-permute-start(bf16[24,32,128]{2,1,0:T(8,128)(2,1)} %get-tuple-element.44), channel_id=1, source_target_pairs={{0,7},{2,0},{4,2},{6,4},{1,6},{3,1},{5,3},{7,5},{8,15},{10,8},{12,... | collective-permute-start | bytes 589832 | tf_op jit(solution)/shard_map/ppermute | solution.py:414
  178.9 9.2 %copy-start.4 = (bf16[24,32,128]{2,1,0:T(8,128)(2,1)}, bf16[24,32,128]{2,1,0:T(8,128)(2,1)S(1)}, u32[]{:S(2)}) copy-start(bf16[24,32,128]{2,1,0:T(8,128)(2,1)S(1)} %collective-permute-done.12.refs_3_) | copy-start | bytes 589828
  178.9 9.2 %copy-start.5 = (bf16[24,32,128]{2,1,0:T(8,128)(2,1)}, bf16[24,32,128]{2,1,0:T(8,128)(2,1)S(1)}, u32[]{:S(2)}) copy-start(bf16[24,32,128]{2,1,0:T(8,128)(2,1)S(1)} %collective-permute-done.13.refs_4_) | copy-start | bytes 589828
  (7 other events, 41.9 us)
